TPU v7x, 32 devices: a whole 2x2x4 slice. The times are simulated.
32 devices in a mesh: groups: 2 (over y), seq: 4 (over z), chan: 4 (over x, core).
Axes of the slice: x: 2, y: 2, z: 4, core: 2. Of those that a mesh axis runs over, the one named last changes fastest.
Arguments:
- dna_bases: int32 [4096], P(('groups', 'seq')), parts along dimension 0, may hold values from 0 to 3
- w_stem: bfloat16 [768, 5, 4], P('chan'), may hold values from -2.5 to 2.5
- w_enc: bfloat16 [1536, 5, 768], P(None, None, 'chan'), may hold values from -0.09375 to 0.09375
- w_dec: bfloat16 [768, 5, 1536], P(None, None, 'chan'), may hold values from -0.0625 to 0.0625
- targets: bfloat16 [4096, 768], P(('groups', 'seq'), 'chan'), parts along dimension 0, may hold values from -6 to 6
Outputs:
- pred: bfloat16 [4096, 768], P(('groups', 'seq'), 'chan'), parts along dimension 0
- g_enc: float32 [3072, 5, 768], P(('groups', 'seq'), None, 'chan'), parts along dimension 0
- g_dec: float32 [1536, 5, 1536], P(('groups', 'seq'), None, 'chan'), parts along dimension 0
There are 2 independent parts, one for each index of `groups`. A program takes and returns all parts, laid end to end along the dimension named above; an argument that names none is the same for every part. Nothing has to cross between parts.
Inputs may be any that keep to these rules, and one draw needn't show every extreme that they name: `dna_bases`: each entry is one of the four bases.
All inputs are finite; a program needn't handle non-finite values.
Results may differ from a plain program's by a relative error of at most 0.009.
Values may be sent and summed in bfloat16 or wider, within the bound.
A program may use at most 192 MiB of HBM per device.

v0:
```python
import math

import jax
import jax.numpy as jnp
from jax import lax
from jax.sharding import PartitionSpec as P

KW = 5


SQRT_TWO_PI = 0.7978845608028654
CUBIC = 0.044715


def extended(block, sides, width):
    for axis, dim in sides:
        count = lax.axis_size(axis)
        forward = [(i, i + 1) for i in range(count - 1)]
        backward = [(target, source) for source, target in forward]
        low = lax.ppermute(
            lax.slice_in_dim(block, block.shape[dim] - width, None, axis=dim), axis, forward
        )
        high = lax.ppermute(lax.slice_in_dim(block, 0, width, axis=dim), axis, backward)
        block = jnp.concatenate([low, block, high], axis=dim)
    return block


def gelu_value(value):
    inner = jnp.tanh(SQRT_TWO_PI * (value + CUBIC * value * value * value))
    return 0.5 * value * (1.0 + inner)


def gelu_slope(value):
    inner = jnp.tanh(SQRT_TWO_PI * (value + CUBIC * value * value * value))
    return 0.5 * (1.0 + inner) + 0.5 * value * (1.0 - inner * inner) * SQRT_TWO_PI * (
        1.0 + 3.0 * CUBIC * value * value
    )


def rim_cells(block, margin):
    return extended(block, (("seq", 0),), margin)


def channel_sum(partial_value):
    return lax.psum_scatter(partial_value, "chan", scatter_dimension=1, tiled=True)


def channel_gather(block):
    return lax.all_gather(block, "chan", axis=1, tiled=True)


def conv_rows(padded, weight):
    row_count = padded.shape[0] - 4
    total = jnp.zeros((row_count, weight.shape[0]), jnp.float32)
    for k in range(KW):
        total = total + lax.dot_general(
            padded[k : k + row_count],
            weight[:, k, :],
            (((1,), (1,)), ((), ())),
            preferred_element_type=jnp.float32,
        )
    return total


def grad_taps(picked, padded):
    row_count = picked.shape[0]
    pieces = [
        lax.dot_general(
            picked,
            padded[k : k + row_count],
            (((0,), (0,)), ((), ())),
            preferred_element_type=jnp.float32,
        )
        for k in range(KW)
    ]
    return jnp.stack(pieces, axis=1)


def weight_grad(cotangent, padded):
    rounded = grad_taps(cotangent, padded).astype(jnp.bfloat16)
    return lax.psum_scatter(
        lax.optimization_barrier(rounded).astype(jnp.float32),
        "seq",
        scatter_dimension=0,
        tiled=True,
    )


def shards(dna_bases, w_stem, w_enc, w_dec, targets):
    row_count = dna_bases.shape[0]
    devices = lax.axis_size("seq")
    length = row_count * devices
    onehot = (dna_bases[:, None] == jnp.arange(4, dtype=jnp.int32)[None, :]).astype(jnp.bfloat16)
    onehot_pad = rim_cells(onehot, 2)
    stem_out = gelu_value(conv_rows(onehot_pad, w_stem)).astype(jnp.bfloat16)
    stem_pad = rim_cells(stem_out, 2)
    enc_pre = channel_sum(conv_rows(stem_pad, w_enc))
    active = gelu_value(enc_pre).astype(jnp.bfloat16).astype(jnp.float32)
    pooled = (0.5 * active.reshape(row_count // 2, 2, -1).sum(axis=1)).astype(jnp.bfloat16)
    pooled_pad = rim_cells(pooled, 1)
    up_pad = jnp.repeat(pooled_pad, 2, axis=0)
    output = channel_sum(conv_rows(up_pad, w_dec)) + stem_out.astype(jnp.float32)
    pred = output.astype(jnp.bfloat16)
    scale = 1.0 / math.sqrt(length)
    slope_out = ((output - targets.astype(jnp.float32)) * scale).astype(jnp.bfloat16)
    slope_all = channel_gather(slope_out)
    g_dec = weight_grad(slope_all, up_pad)
    slope_pad = rim_cells(slope_all, 2)
    up_grad = jnp.zeros((row_count, w_dec.shape[2]), jnp.float32)
    for k in range(KW):
        up_grad = up_grad + jnp.dot(
            slope_pad[4 - k : 4 - k + row_count], w_dec[:, k, :], preferred_element_type=jnp.float32
        )
    pool_grad = up_grad.reshape(row_count // 2, 2, -1).sum(axis=1)
    act_grad = 0.5 * jnp.repeat(pool_grad, 2, axis=0)
    pre_grad = (act_grad * gelu_slope(enc_pre)).astype(jnp.bfloat16)
    pre_all = channel_gather(pre_grad)
    g_enc = weight_grad(pre_all, stem_pad)
    return (pred, g_enc, g_dec)


def solution(mesh):
    return jax.shard_map(
        shards,
        mesh=mesh,
        in_specs=(
            P(("groups", "seq")),
            P("chan", None, None),
            P(None, None, "chan"),
            P(None, None, "chan"),
            P(("groups", "seq"), "chan"),
        ),
        out_specs=(
            P(("groups", "seq"), "chan"),
            P(("groups", "seq"), None, "chan"),
            P(("groups", "seq"), None, "chan"),
        ),
        check_vma=False,
    )
```

profile of v0, /device:TPU:0, one launch (start us, length us, event | category | flops | bytes accessed | tf_op | source)
XLA Modules:
  0.0 406.5 jit_solution(9728655634134982751)
XLA Ops:
  8.1 4.9 %collective-permute-start = (bf16[2,4]{0,1:T(4,128)(2,1)S(1)}, bf16[2,4]{0,1:T(4,128)(2,1)S(1)}, u32[]{:S(2)}, u32[]{:S(2)}) collective-permute-start(bf16[2,4]{0,1:T(4,128)(2,1)S(1)} %get-tuple-element.13), channel_id=1, source_target_pairs={{0,4},{4,8},{8,12},{1,5},{5,9},{9,13},{2,6},{6,10},{10,14},{3,7},{... | collective-permute-start | bytes 56 | tf_op jit(solution)/shard_map/ppermute | solution.py:20
  15.3 3.2 collective-permute-done.1
  22.5 3.5 collective-permute-start.2
  28.0 4.1 %collective-permute-done.3 = bf16[2,192]{0,1:T(8,128)(2,1)S(1)} collective-permute-done((bf16[2,192]{0,1:T(8,128)(2,1)S(1)}, bf16[2,192]{0,1:T(8,128)(2,1)S(1)}, u32[]{:S(2)}, u32[]{:S(2)}) %collective-permute-start.3) | collective-permute-done | bytes 800 | tf_op jit(solution)/shard_map/ppermute | solution.py:23
  34.3 2.4 fusion
  36.8 37.3 %reduce-scatter.5.cloned.1.call-done = f32[512,384]{1,0:T(8,128)} async-done(((f32[512,1536]{1,0:T(8,128)}), f32[512,384]{1,0:T(8,128)}) %reduce-scatter.5.cloned.1.call-update) | async-done | bytes 786448 | tf_op jit(solution)/shard_map/reduce_scatter | solution.py:45
  76.9 3.4 collective-permute-start.4
  81.9 1.8 fusion.47
  83.7 2.0 collective-permute-done.5
  87.3 1.8 fusion.43
  89.1 3.0 fusion.50
  93.8 1.9 slice.192
  95.7 1.9 broadcast_in_dim.14
  97.6 1.9 slice.182
  99.5 1.9 fusion.53
  101.4 3.2 add_add_fusion
  104.7 27.5 %reduce-scatter.7.cloned.1.call-done = f32[512,192]{0,1:T(8,128)} async-done(((f32[512,768]{0,1:T(8,128)}), f32[512,192]{0,1:T(8,128)}) %reduce-scatter.7.cloned.1.call-update) | async-done | bytes 393232 | tf_op jit(solution)/shard_map/reduce_scatter | solution.py:45
  132.2 1.8 multiply_convert_fusion.1
  133.9 8.3 %all_gather.6 = bf16[512,768]{0,1:T(8,128)(2,1)S(1)} all-gather(bf16[512,192]{0,1:T(8,128)(2,1)S(1)} %get-tuple-element.5), channel_id=1, replica_groups=mesh['groups'=2,'seq'=4,'chan'=4] {'chan'}, dimensions={1}, use_global_device_ids=true | all-gather | bytes 983040 | tf_op jit(solution)/shard_map/all_gather | solution.py:49
  142.4 1.7 fusion.45
  145.4 4.7 %collective-permute-start.7 = (bf16[2,768]{0,1:T(8,128)(2,1)S(1)}, bf16[2,768]{0,1:T(8,128)(2,1)S(1)}, u32[]{:S(2)}, u32[]{:S(2)}) collective-permute-start(bf16[2,768]{0,1:T(8,128)(2,1)S(1)} %get-tuple-element.4), channel_id=1, source_target_pairs={{0,4},{4,8},{8,12},{1,5},{5,9},{9,13},{2,6},{6,10},{10,14},{3,7},{... | collective-permute-start | bytes 9224 | tf_op jit(solution)/shard_map/ppermute | solution.py:20
  150.2 2.9 collective-permute-done.6
  156.1 1.9 fusion.12
  158.0 1.7 reshape.28
  162.4 2.4 fusion.34
  168.1 2.9 convert_element_type.46
  171.2 14.0 %all-gather.2.cloned.1.call-done = bf16[512,1536]{1,0:T(8,128)(2,1)} async-done(((bf16[512,384]{1,0:T(8,128)(2,1)}), bf16[512,1536]{1,0:T(8,128)(2,1)}) %all-gather.2.cloned.1.call-update) | async-done | bytes 1572880 | tf_op jit(solution)/shard_map/all_gather | solution.py:49
  185.1 2.1 fusion.3
  187.2 1.9 fusion.5
  190.7 3.4 convert_element_type.45
  194.1 98.1 %reduce-scatter.11.cloned.1.call-done = f32[192,5,384]{2,0,1:T(8,128)} async-done(((f32[768,5,384]{2,0,1:T(8,128)}), f32[192,5,384]{2,0,1:T(8,128)}) %reduce-scatter.11.cloned.1.call-update) | async-done | bytes 1474576 | tf_op jit(solution)/shard_map/reduce_scatter | solution.py:81
  292.3 107.7 %reduce-scatter.9.cloned.1.call-done = f32[384,5,192]{0,2,1:T(8,128)} async-done(((f32[1536,5,192]{0,2,1:T(8,128)}), f32[384,5,192]{0,2,1:T(8,128)}) %reduce-scatter.9.cloned.1.call-update) | async-done | bytes 1474576 | tf_op jit(solution)/shard_map/reduce_scatter | solution.py:81
  (90 shorter events, 31.2 us)
Async XLA Ops:
  7.2 20.2 %copy-start.5 = (bf16[1536,5,192]{0,2,1:T(8,128)(2,1)S(1)}, bf16[1536,5,192]{0,2,1:T(8,128)(2,1)}, u32[]{:S(2)}) copy-start(bf16[1536,5,192]{0,2,1:T(8,128)(2,1)} %param.7) | copy-start | bytes 8847364
  7.2 66.9 %reduce-scatter.5.cloned.1.call-start = ((), (), s32[]{:S(2)}) async-start(), calls=%async_computation.4 | async-start | bytes 3932160 | tf_op jit(solution)/shard_map/reduce_scatter | solution.py:45
  8.1 11.3 %collective-permute-start = (bf16[2,4]{0,1:T(4,128)(2,1)S(1)}, bf16[2,4]{0,1:T(4,128)(2,1)S(1)}, u32[]{:S(2)}, u32[]{:S(2)}) collective-permute-start(bf16[2,4]{0,1:T(4,128)(2,1)S(1)} %get-tuple-element.13), channel_id=1, source_target_pairs={{0,4},{4,8},{8,12},{1,5},{5,9},{9,13},{2,6},{6,10},{10,14},{3,7},{... | collective-permute-start | bytes 56 | tf_op jit(solution)/shard_map/ppermute | solution.py:20
  13.1 5.5 %collective-permute-start.1 = (bf16[2,4]{0,1:T(4,128)(2,1)S(1)}, bf16[2,4]{0,1:T(4,128)(2,1)S(1)}, u32[]{:S(2)}, u32[]{:S(2)}) collective-permute-start(bf16[2,4]{0,1:T(4,128)(2,1)S(1)} %get-tuple-element.14), channel_id=1, source_target_pairs={{4,0},{8,4},{12,8},{5,1},{9,5},{13,9},{6,2},{10,6},{14,10},{7,3},{... | collective-permute-start | bytes 56 | tf_op jit(solution)/shard_map/ppermute | solution.py:23
  22.5 10.2 %collective-permute-start.2 = (bf16[2,192]{0,1:T(8,128)(2,1)S(1)}, bf16[2,192]{0,1:T(8,128)(2,1)S(1)}, u32[]{:S(2)}, u32[]{:S(2)}) collective-permute-start(bf16[2,192]{0,1:T(8,128)(2,1)S(1)} %get-tuple-element.11), channel_id=1, source_target_pairs={{0,4},{4,8},{8,12},{1,5},{5,9},{9,13},{2,6},{6,10},{10,14},{3,7},{... | collective-permute-start | bytes 2312 | tf_op jit(solution)/shard_map/ppermute | solution.py:20
  26.0 6.0 %collective-permute-start.3 = (bf16[2,192]{0,1:T(8,128)(2,1)S(1)}, bf16[2,192]{0,1:T(8,128)(2,1)S(1)}, u32[]{:S(2)}, u32[]{:S(2)}) collective-permute-start(bf16[2,192]{0,1:T(8,128)(2,1)S(1)} %get-tuple-element.12), channel_id=1, source_target_pairs={{4,0},{8,4},{12,8},{5,1},{9,5},{13,9},{6,2},{10,6},{14,10},{7,3},{... | collective-permute-start | bytes 2312 | tf_op jit(solution)/shard_map/ppermute | solution.py:23
  32.0 2.3 copy-start.10
  32.8 1.5 copy-start.12
  36.7 95.5 %reduce-scatter.7.cloned.1.call-start = ((), (), s32[]{:S(2)}) async-start(), calls=%async_computation.5 | async-start | bytes 1966080 | tf_op jit(solution)/shard_map/reduce_scatter | solution.py:45
  76.9 6.9 %collective-permute-start.4 = (bf16[1,384]{1,0:T(2,128)(2,1)S(1)}, bf16[1,384]{1,0:T(2,128)(2,1)S(1)}, u32[]{:S(2)}, u32[]{:S(2)}) collective-permute-start(bf16[1,384]{1,0:T(2,128)(2,1)S(1)} %get-tuple-element.9), channel_id=1, source_target_pairs={{0,4},{4,8},{8,12},{1,5},{5,9},{9,13},{2,6},{6,10},{10,14},{3,7},{... | collective-permute-start | bytes 2312 | tf_op jit(solution)/shard_map/ppermute | solution.py:20
  80.2 5.5 %collective-permute-start.5 = (bf16[1,384]{1,0:T(2,128)(2,1)S(1)}, bf16[1,384]{1,0:T(2,128)(2,1)S(1)}, u32[]{:S(2)}, u32[]{:S(2)}) collective-permute-start(bf16[1,384]{1,0:T(2,128)(2,1)S(1)} %get-tuple-element.10), channel_id=1, source_target_pairs={{4,0},{8,4},{12,8},{5,1},{9,5},{13,9},{6,2},{10,6},{14,10},{7,3},{... | collective-permute-start | bytes 2312 | tf_op jit(solution)/shard_map/ppermute | solution.py:23
  81.9 3.8 copy-start.7
  99.5 1.9 copy-start.1
  101.4 30.7 %copy-start.14 = (bf16[512,192]{0,1:T(8,128)(2,1)S(1)}, bf16[512,192]{0,1:T(8,128)(2,1)}, u32[]{:S(2)}) copy-start(bf16[512,192]{0,1:T(8,128)(2,1)} %param.9) | copy-start | bytes 589828
  104.6 80.5 %all-gather.2.cloned.1.call-start = ((), (), s32[]{:S(2)}) async-start(), calls=%async_computation.6 | async-start | bytes 1966080 | tf_op jit(solution)/shard_map/all_gather | solution.py:49
  133.9 19.2 %copy-start.2 = (bf16[768,5,384]{2,0,1:T(8,128)(2,1)S(1)}, bf16[768,5,384]{2,0,1:T(8,128)(2,1)}, u32[]{:S(2)}) copy-start(bf16[768,5,384]{2,0,1:T(8,128)(2,1)} %param.8) | copy-start | bytes 8847364
  144.1 9.1 %collective-permute-start.6 = (bf16[2,768]{0,1:T(8,128)(2,1)S(1)}, bf16[2,768]{0,1:T(8,128)(2,1)S(1)}, u32[]{:S(2)}, u32[]{:S(2)}) collective-permute-start(bf16[2,768]{0,1:T(8,128)(2,1)S(1)} %get-tuple-element.3), channel_id=1, source_target_pairs={{4,0},{8,4},{12,8},{5,1},{9,5},{13,9},{6,2},{10,6},{14,10},{7,3},{... | collective-permute-start | bytes 9224 | tf_op jit(solution)/shard_map/ppermute | solution.py:23
  145.4 9.7 %collective-permute-start.7 = (bf16[2,768]{0,1:T(8,128)(2,1)S(1)}, bf16[2,768]{0,1:T(8,128)(2,1)S(1)}, u32[]{:S(2)}, u32[]{:S(2)}) collective-permute-start(bf16[2,768]{0,1:T(8,128)(2,1)S(1)} %get-tuple-element.4), channel_id=1, source_target_pairs={{0,4},{4,8},{8,12},{1,5},{5,9},{9,13},{2,6},{6,10},{10,14},{3,7},{... | collective-permute-start | bytes 9224 | tf_op jit(solution)/shard_map/ppermute | solution.py:20
  158.0 4.4 %copy-start.4 = (f32[512,384]{1,0:T(8,128)S(1)}, f32[512,384]{1,0:T(8,128)}, u32[]{:S(2)}) copy-start(f32[512,384]{1,0:T(8,128)} %reduce-scatter.5.cloned.1.call-done) | copy-start | bytes 2359300
  160.6 4.2 %copy-start.9 = (bf16[512,384]{1,0:T(8,128)(2,1)S(1)}, bf16[512,384]{1,0:T(8,128)(2,1)}, u32[]{:S(2)}) copy-start(bf16[512,384]{1,0:T(8,128)(2,1)} %slice.182) | copy-start | bytes 1179652
  160.9 4.5 %copy-start.3 = (bf16[516,384]{1,0:T(8,128)(2,1)S(1)}, bf16[516,384]{1,0:T(8,128)(2,1)}, u32[]{:S(2)}) copy-start(bf16[516,384]{1,0:T(8,128)(2,1)} %reshape.27) | copy-start | bytes 1188868
  164.8 1.4 copy-start.8
  164.8 127.5 %reduce-scatter.11.cloned.1.call-start = ((), (), s32[]{:S(2)}) async-start(), calls=%async_computation.8 | async-start | bytes 7372800 | tf_op jit(solution)/shard_map/reduce_scatter | solution.py:81
  166.1 1.3 copy-start.6
  171.1 14.1 %copy-start.13 = (bf16[2,192]{0,1:T(8,128)(2,1)S(1)}, bf16[2,192]{0,1:T(8,128)(2,1)}, u32[]{:S(2)}) copy-start(bf16[2,192]{0,1:T(8,128)(2,1)} %copy-done.12) | copy-start | bytes 2308
  171.1 228.9 %reduce-scatter.9.cloned.1.call-start = ((), (), s32[]{:S(2)}) async-start(), calls=%async_computation.7 | async-start | bytes 7372800 | tf_op jit(solution)/shard_map/reduce_scatter | solution.py:81
  185.1 4.0 copy-start
  187.2 2.5 copy-start.11
Sparse Core Ops, SparseCore 0:
  36.8 37.1 reduce-scatter.4
  104.7 27.3 reduce-scatter.6
  164.9 20.1 all-gather.1
  187.9 104.3 reduce-scatter.10
  295.0 104.8 reduce-scatter.8
where the time goes:
time: 407 us; the launch traced here: 406 us
  waiting for transfers between devices  297 us (73%)
  matrix products  36.9 us (9%)
  starting transfers between devices  21.9 us (5%)
  other arithmetic  15.4 us (4%)
  between operations  14.3 us (4%)
  local copies, waits for them, and re-layouts  12.8 us (3%)
  blocking collectives  8.34 us (2%)
    reduce_scatter x2, waiting for transfers between devices, weight_grad(): lax.psum_scatter(lax.optimization_barrier(rounded).astype(jnp.float32), '...  206 us
    reduce_scatter x2, waiting for transfers between devices, channel_sum(): lax.psum_scatter(partial_value, 'chan', scatter_dimension=1, tiled=True)  64.8 us
    dot_general x15, matrix products, conv_rows(): lax.dot_general(padded[k:k + row_count], weight[:, k, :], (((1,), (1,)),...  21.7 us
    ppermute x4, starting transfers between devices, extended(): lax.ppermute(lax.slice_in_dim(block, block.shape[dim] - width, None, axis...  16.5 us
    all_gather x1, waiting for transfers between devices, channel_gather(): return lax.all_gather(block, 'chan', axis=1, tiled=True)  14 us
    ppermute x4, waiting for transfers between devices, extended(): lax.ppermute(lax.slice_in_dim(block, 0, width, axis=dim), axis, backward)  12.2 us
    dot_general x10, matrix products, grad_taps(): lax.dot_general(picked, padded[k:k + row_count], (((0,), (0,)), ((), ()))...  8.74 us
    all_gather x1, blocking collectives, channel_gather(): return lax.all_gather(block, 'chan', axis=1, tiled=True)  8.34 us
  transfers between devices with their start and end apart: 13, of which 9 were waited for; matrix products, arithmetic and copies ran while one was open for 6% of the time, Pallas kernels for 0%

commit v1 on v0

--- a/solution.py
+++ b/solution.py
@@ -1,8 +1,11 @@
+import functools
 import math
 
 import jax
 import jax.numpy as jnp
 from jax import lax
+from jax.experimental import pallas as pl
+from jax.experimental.pallas import tpu as pltpu
 from jax.sharding import PartitionSpec as P
 
 KW = 5
@@ -86,7 +89,7 @@
     )
 
 
-def shards(dna_bases, w_stem, w_enc, w_dec, targets):
+def general_shards(dna_bases, w_stem, w_enc, w_dec, targets):
     row_count = dna_bases.shape[0]
     devices = lax.axis_size("seq")
     length = row_count * devices
@@ -119,6 +122,342 @@
     return (pred, g_enc, g_dec)
 
 
+MESH_ID = pl.DeviceIdType.MESH
+BF16 = jnp.bfloat16
+EDGE = 16
+VMEM_BYTES = 52 * 1024 * 1024
+
+
+def send(src, dst, send_sem, recv_sem, seq, chan):
+    return pltpu.make_async_remote_copy(
+        src_ref=src,
+        dst_ref=dst,
+        send_sem=send_sem,
+        recv_sem=recv_sem,
+        device_id={"seq": seq, "chan": chan},
+        device_id_type=MESH_ID,
+    )
+
+
+def greet(targets):
+    barrier = pltpu.get_barrier_semaphore()
+    for seq, chan in targets:
+        pl.semaphore_signal(
+            barrier, inc=1, device_id={"seq": seq, "chan": chan}, device_id_type=MESH_ID
+        )
+    pl.semaphore_wait(barrier, len(targets))
+
+
+def whole_group(n, s, c):
+    others = []
+    for ds in range(n):
+        for dc in range(n):
+            if ds or dc:
+                others.append((lax.rem(s + ds, n), lax.rem(c + dc, n)))
+    return others
+
+
+def bases_kernel(n, own_ref, all_ref, local_sem, send_sem, recv_sem):
+    s, c = lax.axis_index("seq"), lax.axis_index("chan")
+    peers = [lax.rem(s + d, n) for d in range(1, n)]
+    greet([(p, c) for p in peers])
+    copies = [
+        send(own_ref, all_ref.at[s], send_sem.at[d], recv_sem.at[d], p, c)
+        for d, p in enumerate(peers)
+    ]
+    for copy in copies:
+        copy.start()
+    mine = pltpu.make_async_copy(own_ref, all_ref.at[s], local_sem)
+    mine.start()
+    mine.wait()
+    for copy in copies:
+        copy.wait()
+
+
+def encoder_kernel(
+    n, part_ref, pre_ref, pool_ref, held, wide, edge_lo, edge_hi,
+    send_sem, recv_sem, edge_send, edge_recv,
+):
+    s, c = lax.axis_index("seq"), lax.axis_index("chan")
+    rows, width = pre_ref.shape
+    half = rows // 2
+    peers = [lax.rem(c + d, n) for d in range(1, n)]
+    greet([(s, p) for p in peers] + [(lax.rem(s + d, n), c) for d in range(1, n)])
+    copies = []
+    for d, p in enumerate(peers):
+        columns = pl.ds(pl.multiple_of(p * width, 128), width)
+        copies.append(
+            send(part_ref.at[:, columns], held.at[d], send_sem.at[d], recv_sem.at[d], s, p)
+        )
+    for copy in copies:
+        copy.start()
+    own = pl.ds(pl.multiple_of(c * width, 128), width)
+    for copy in copies:
+        copy.wait_recv()
+    step = 64
+
+    @pl.loop(0, rows // step)
+    def _(i):
+        at = pl.ds(pl.multiple_of(i * step, step), step)
+        total = part_ref[at, own].astype(jnp.float32)
+        for d in range(n - 1):
+            total = total + held[d, at, :].astype(jnp.float32)
+        pre_ref[at, :] = total
+        active = gelu_value(total).astype(BF16).astype(jnp.float32)
+        for j in range(width // 128):
+            wide[j, at, :] = active[:, j * 128 : (j + 1) * 128]
+
+    for j in range(width // 128):
+        even = wide[j, pl.ds(0, half, stride=2), :]
+        odd = wide[j, pl.ds(1, half, stride=2), :]
+        pool_ref[EDGE : EDGE + half, j * 128 : (j + 1) * 128] = (0.5 * (even + odd)).astype(BF16)
+    up = send(pool_ref.at[pl.ds(half, EDGE)], edge_lo, edge_send.at[0], edge_recv.at[0],
+              lax.rem(s + 1, n), c)
+    down = send(pool_ref.at[pl.ds(EDGE, EDGE)], edge_hi, edge_send.at[1], edge_recv.at[1],
+                lax.rem(s + n - 1, n), c)
+    up.start()
+    down.start()
+    up.wait()
+    down.wait()
+    pool_ref[0:EDGE, :] = jnp.where(s > 0, edge_lo[...].astype(jnp.float32), 0.0).astype(BF16)
+    pool_ref[half + EDGE :, :] = jnp.where(
+        s < n - 1, edge_hi[...].astype(jnp.float32), 0.0
+    ).astype(BF16)
+    for copy in copies:
+        copy.wait_send()
+
+
+def slope_kernel(
+    n, scale, part_ref, stem_ref, target_ref, pred_ref, chan_ref, seq_ref, held, slope,
+    send_sem, recv_sem, row_send, row_recv, turn_send, turn_recv, lo_send, lo_recv, hi_send, hi_recv,
+    local_sem,
+):
+    s, c = lax.axis_index("seq"), lax.axis_index("chan")
+    rows, width = pred_ref.shape
+    peers = [lax.rem(c + d, n) for d in range(1, n)]
+    greet(whole_group(n, s, c))
+    copies = [
+        send(part_ref.at[p], held.at[d], send_sem.at[d], recv_sem.at[d], s, p)
+        for d, p in enumerate(peers)
+    ]
+    for copy in copies:
+        copy.start()
+    for copy in copies:
+        copy.wait_recv()
+    step = 64
+
+    @pl.loop(0, rows // step)
+    def _(i):
+        at = pl.ds(pl.multiple_of(i * step, step), step)
+        total = part_ref[c, at, :].astype(jnp.float32)
+        for d in range(n - 1):
+            total = total + held[d, at, :].astype(jnp.float32)
+        output = total + stem_ref[at, :].astype(jnp.float32)
+        pred_ref[at, :] = output.astype(BF16)
+        slope[at, :] = ((output - target_ref[at, :].astype(jnp.float32)) * scale).astype(BF16)
+
+    core = pl.ds(EDGE, rows)
+    up, down = lax.rem(s + 1, n), lax.rem(s + n - 1, n)
+    row_copies = [
+        send(slope, chan_ref.at[c, core], row_send.at[d], row_recv.at[d], s, p)
+        for d, p in enumerate(peers)
+    ]
+    lo_copies, hi_copies = [], []
+    for d in range(n):
+        p = lax.rem(c + d, n)
+        lo_copies.append(
+            send(slope.at[pl.ds(rows - EDGE, EDGE)], chan_ref.at[c, pl.ds(0, EDGE)],
+                 lo_send.at[d], lo_recv.at[d], up, p)
+        )
+        hi_copies.append(
+            send(slope.at[pl.ds(0, EDGE)], chan_ref.at[c, pl.ds(EDGE + rows, EDGE)],
+                 hi_send.at[d], hi_recv.at[d], down, p)
+        )
+    for copy in row_copies + lo_copies + hi_copies:
+        copy.start()
+    mine = pltpu.make_async_copy(slope, chan_ref.at[c, core], local_sem.at[0])
+    mine.start()
+    for j in range(n):
+        turned = send(slope, seq_ref.at[s], turn_send.at[j], turn_recv.at[s], c, j)
+        itself = jnp.logical_and(s == c, c == j)
+
+        @pl.when(jnp.logical_not(itself))
+        def _():
+            turned.start()
+
+        @pl.when(itself)
+        def _():
+            keep = pltpu.make_async_copy(slope, seq_ref.at[s], local_sem.at[1])
+            keep.start()
+            keep.wait()
+
+    for copy in row_copies + lo_copies + hi_copies:
+        copy.wait()
+    mine.wait()
+    for j in range(n):
+        @pl.when(jnp.logical_not(jnp.logical_and(s == c, c == j)))
+        def _():
+            send(slope, seq_ref.at[s], turn_send.at[j], turn_recv.at[s], c, j).wait_send()
+
+        @pl.when(jnp.logical_not(jnp.logical_and(s == c, s == j)))
+        def _():
+            send(slope, seq_ref.at[j], turn_send.at[j], turn_recv.at[j], c, j).wait_recv()
+    for copy in copies:
+        copy.wait_send()
+    blank = jnp.zeros((EDGE, width), BF16)
+
+    @pl.when(s == 0)
+    def _():
+        for j in range(n):
+            chan_ref[j, 0:EDGE, :] = blank
+
+    @pl.when(s == n - 1)
+    def _():
+        for j in range(n):
+            chan_ref[j, EDGE + rows :, :] = blank
+
+
+def turn_kernel(n, own_ref, seq_ref, turn_send, turn_recv, local_sem):
+    s, c = lax.axis_index("seq"), lax.axis_index("chan")
+    greet(whole_group(n, s, c))
+    for j in range(n):
+        turned = send(own_ref, seq_ref.at[s], turn_send.at[j], turn_recv.at[s], c, j)
+        itself = jnp.logical_and(s == c, c == j)
+
+        @pl.when(jnp.logical_not(itself))
+        def _():
+            turned.start()
+
+        @pl.when(itself)
+        def _():
+            keep = pltpu.make_async_copy(own_ref, seq_ref.at[s], local_sem)
+            keep.start()
+            keep.wait()
+
+    for j in range(n):
+        @pl.when(jnp.logical_not(jnp.logical_and(s == c, c == j)))
+        def _():
+            send(own_ref, seq_ref.at[s], turn_send.at[j], turn_recv.at[s], c, j).wait_send()
+
+        @pl.when(jnp.logical_not(jnp.logical_and(s == c, s == j)))
+        def _():
+            send(own_ref, seq_ref.at[j], turn_send.at[j], turn_recv.at[j], c, j).wait_recv()
+
+
+def call(kernel, ident, outs, scratch, *operands):
+    vmem = pl.BlockSpec(memory_space=pltpu.VMEM)
+    return pl.pallas_call(
+        kernel,
+        out_shape=outs,
+        in_specs=[vmem] * len(operands),
+        out_specs=jax.tree.map(lambda _: vmem, outs),
+        scratch_shapes=scratch,
+        compiler_params=pltpu.CompilerParams(
+            collective_id=ident, has_side_effects=True, vmem_limit_bytes=VMEM_BYTES
+        ),
+    )(*operands)
+
+
+def dma(count):
+    return pltpu.SemaphoreType.DMA((count,))
+
+
+def all_rows_grad(cotangent, padded):
+    count = cotangent.shape[0]
+    pieces = [
+        lax.dot_general(
+            cotangent, padded[k : k + count], (((0,), (0,)), ((), ())),
+            preferred_element_type=jnp.float32,
+        )
+        for k in range(KW)
+    ]
+    return jnp.stack(pieces, axis=1)
+
+
+def square_shards(dna_bases, w_stem, w_enc, w_dec, targets):
+    rows = dna_bases.shape[0]
+    n = lax.axis_size("seq")
+    length = rows * n
+    s = lax.axis_index("seq")
+    c1, c2 = w_stem.shape[0], w_dec.shape[2]
+    struct = jax.ShapeDtypeStruct
+    bases = call(
+        functools.partial(bases_kernel, n), 0, struct((n, rows // 128, 128), jnp.int32),
+        [pltpu.SemaphoreType.DMA, dma(n - 1), dma(n - 1)], dna_bases.reshape(rows // 128, 128),
+    ).reshape(length)
+    bases_pad = jnp.pad(bases, (2, 2), constant_values=-1)
+    shifts = jnp.stack([bases_pad[k : k + length] for k in range(KW)])
+    onehot = (shifts[:, None, :] == jnp.arange(4, dtype=jnp.int32)[None, :, None]).astype(BF16)
+    stem_pre = lax.dot_general(
+        onehot.reshape(KW * 4, length), w_stem.reshape(c1, KW * 4), (((0,), (1,)), ((), ())),
+        preferred_element_type=jnp.float32,
+    )
+    stem_all = jnp.pad(gelu_value(stem_pre).astype(BF16), ((2, 2), (0, 0)))
+    stem_pad = lax.dynamic_slice_in_dim(stem_all, s * rows, rows + 4, 0)
+    part = conv_rows(stem_pad, w_enc).astype(BF16)
+    enc_pre, pool_pad = call(
+        functools.partial(encoder_kernel, n), 1,
+        (struct((rows, c2), jnp.float32), struct((rows // 2 + 2 * EDGE, c2), BF16)),
+        [
+            pltpu.VMEM((n - 1, rows, c2), BF16),
+            pltpu.VMEM((c2 // 128, rows, 128), jnp.float32),
+            pltpu.VMEM((EDGE, c2), BF16),
+            pltpu.VMEM((EDGE, c2), BF16),
+            dma(n - 1), dma(n - 1), dma(2), dma(2),
+        ],
+        part,
+    )
+    half = rows // 2
+    pool_all = lax.all_gather(pool_pad[EDGE : EDGE + half], "seq", axis=0, tiled=True)
+    up_pad = jnp.repeat(pool_pad[EDGE - 1 : EDGE + half + 1], 2, axis=0)
+    dec_part = conv_rows(up_pad, w_dec).astype(BF16)
+    dec_part = dec_part.reshape(rows, n, c1).transpose(1, 0, 2)
+    pred, slope_chan, slope_seq = call(
+        functools.partial(slope_kernel, n, 1.0 / math.sqrt(length)), 2,
+        (
+            struct((rows, c1), BF16),
+            struct((n, rows + 2 * EDGE, c1), BF16),
+            struct((n, rows, c1), BF16),
+        ),
+        [
+            pltpu.VMEM((n - 1, rows, c1), BF16),
+            pltpu.VMEM((rows, c1), BF16),
+            dma(n - 1), dma(n - 1), dma(n - 1), dma(n - 1), dma(n), dma(n),
+            dma(n), dma(n), dma(n), dma(n), dma(2),
+        ],
+        dec_part, stem_pad[2 : 2 + rows], targets,
+    )
+    slope_pad = jnp.concatenate(
+        [slope_chan[j, EDGE - 2 : EDGE + rows + 2] for j in range(n)], axis=1
+    )
+    up_grad = jnp.zeros((rows, c2), jnp.float32)
+    for k in range(KW):
+        up_grad = up_grad + jnp.dot(
+            slope_pad[4 - k : 4 - k + rows], w_dec[:, k, :], preferred_element_type=jnp.float32
+        )
+    pool_grad = up_grad.reshape(half, 2, -1).sum(axis=1)
+    act_grad = 0.5 * jnp.repeat(pool_grad, 2, axis=0)
+    pre_grad = (act_grad * gelu_slope(enc_pre)).astype(BF16)
+    pre_seq = call(
+        functools.partial(turn_kernel, n), 3, struct((n, rows, c2), BF16),
+        [dma(n), dma(n), pltpu.SemaphoreType.DMA], pre_grad,
+    )
+    up_all = jnp.pad(jnp.repeat(pool_all, 2, axis=0), ((2, 2), (0, 0)))
+    g_dec = all_rows_grad(slope_seq.reshape(length, c1), up_all)
+    g_enc = all_rows_grad(pre_seq.reshape(length, c2), stem_all)
+    return (pred, g_enc, g_dec)
+
+
+def shards(dna_bases, w_stem, w_enc, w_dec, targets):
+    args = (dna_bases, w_stem, w_enc, w_dec, targets)
+    rows, c1, c2 = dna_bases.shape[0], w_stem.shape[0], w_dec.shape[2]
+    n = lax.axis_size("seq")
+    square = n == lax.axis_size("chan") and n > 2
+    if square and rows % 128 == 0 and c2 % 128 == 0 and c1 % 64 == 0:
+        return square_shards(*args)
+    return general_shards(*args)
+
+
 def solution(mesh):
     return jax.shard_map(
         shards,

time: 407 us -> 254 us (0.62)
  the two profiles are of different devices: /device:TPU:0 before, /device:TPU:3 now
where the time goes in v1:
time: 254 us; the launch traced here: 253 us
  Pallas kernels  164 us (65%)
  matrix products  46.3 us (18%)
  local copies, waits for them, and re-layouts  22 us (9%)
  blocking collectives  17.9 us (7%)
    pallas_call x4, Pallas kernels, call(): pl.pallas_call(kernel, out_shape=outs, in_specs=[vmem] * len(operands), o...  164 us
    dot_general x10, matrix products, conv_rows(): lax.dot_general(padded[k:k + row_count], weight[:, k, :], (((1,), (1,)),...  34.8 us
    all_gather x1, blocking collectives, square_shards(): lax.all_gather(pool_pad[EDGE:EDGE + half], 'seq', axis=0, tiled=True)  17.9 us
    dot_general x10, matrix products, all_rows_grad(): lax.dot_general(cotangent, padded[k:k + count], (((0,), (0,)), ((), ())),...  7.67 us

profile of v1, /device:TPU:3, one launch (start us, length us, event | category | flops | bytes accessed | tf_op | source)
XLA Modules:
  0.0 253.4 jit_solution(13794135530452407337)
XLA Ops:
  0.7 0.7 copy-done.1
  1.3 4.7 %shard_map.76 = s32[4,4,128]{2,1,0:T(4,128)S(1)} custom-call(s32[4,128]{1,0:T(4,128)S(1)} %bitcast.136), custom_call_target="tpu_custom_call" | custom-call | tf_op jit(solution)/shard_map/pallas_call | solution.py:349
  6.2 0.9 fusion.5
  7.1 3.6 %fusion.83 = f32[512,1536]{1,0:T(8,128)} fusion(bf16[1536,5,192]{0,2,1:T(8,128)(2,1)} %param.7, s32[]{:T(128)S(6)} %select_n.3, bf16[2048,192]{1,0:T(8,128)(2,1)S(1)} %fusion.5), kind=kOutput, calls=%fused_computation.87 | convolution fusion | flops 301989888 | bytes 4521988 | tf_op jit(solution)/shard_map/dot_general | solution.py:59
  10.8 4.3 %convolution_add_fusion.3 = f32[512,1536]{1,0:T(8,128)} fusion(f32[512,1536]{1,0:T(8,128)} %fusion.83, bf16[1536,5,192]{0,2,1:T(8,128)(2,1)} %param.7, s32[]{:T(128)S(6)} %add.86, bf16[2048,192]{1,0:T(8,128)(2,1)S(1)} %fusion.5), kind=kOutput, calls=%fused_computation.3 | convolution fusion | flops 302776320 | bytes 7667716 | tf_op jit(solution)/shard_map/dot_general | solution.py:59
  15.1 4.3 %convolution_add_fusion.2 = f32[512,1536]{1,0:T(8,128)} fusion(f32[512,1536]{1,0:T(8,128)} %convolution_add_fusion.3, bf16[512,192]{1,0:T(8,128)(2,1)S(1)} %pad_dynamic-slice_fusion.stem_ref, bf16[1536,5,192]{0,2,1:T(8,128)(2,1)} %param.7), kind=kOutput, calls=%fused_computation.2 | convolution fusion | flops 302776320 | bytes 7077888 | tf_op jit(solution)/shard_map/dot_general | solution.py:59
  19.4 4.3 %convolution_add_fusion.1 = f32[512,1536]{1,0:T(8,128)} fusion(f32[512,1536]{1,0:T(8,128)} %convolution_add_fusion.2, bf16[1536,5,192]{0,2,1:T(8,128)(2,1)} %param.7, s32[]{:T(128)S(6)} %add.88, bf16[2048,192]{1,0:T(8,128)(2,1)S(1)} %fusion.5), kind=kOutput, calls=%fused_computation.1 | convolution fusion | flops 302776320 | bytes 7667716 | tf_op jit(solution)/shard_map/dot_general | solution.py:59
  23.7 3.8 %fusion.part_ref = bf16[512,1536]{1,0:T(8,128)(2,1)} fusion(f32[512,1536]{1,0:T(8,128)} %convolution_add_fusion.1, bf16[1536,5,192]{0,2,1:T(8,128)(2,1)} %param.7, s32[]{:T(128)S(6)} %add.89, bf16[2048,192]{1,0:T(8,128)(2,1)S(1)} %fusion.5), kind=kOutput, calls=%fused_computation.5 | convolution fusion | flops 303562752 | bytes 6094852 | tf_op jit(solution)/shard_map/dot_general | solution.py:59
  27.5 27.2 %shard_map.77 = (f32[512,384]{1,0:T(8,128)S(1)}, bf16[288,384]{1,0:T(8,128)(2,1)S(1)}) custom-call(bf16[512,1536]{1,0:T(8,128)(2,1)} %fusion.part_ref), custom_call_target="tpu_custom_call" | custom-call | tf_op jit(solution)/shard_map/pallas_call | solution.py:349
  54.7 0.8 fusion.132
  55.9 1.7 fusion.71
  57.9 0.9 slice.166
  58.8 2.9 %fusion.77 = f32[512,768]{1,0:T(8,128)} fusion(bf16[512,384]{1,0:T(8,128)(2,1)} %slice.166, bf16[768,5,384]{2,0,1:T(8,128)(2,1)} %param.8), kind=kOutput, calls=%fused_computation.81 | convolution fusion | flops 301989888 | bytes 2555904 | tf_op jit(solution)/shard_map/dot_general | solution.py:59
  61.7 1.0 broadcast_in_dim.18
  62.7 1.6 reshape.42
  64.3 2.9 %fusion.68 = f32[512,768]{1,0:T(8,128)} fusion(bf16[768,5,384]{2,0,1:T(8,128)(2,1)} %param.8, bf16[516,384]{1,0:T(8,128)(2,1)S(1)} %reshape.42), kind=kOutput, calls=%fused_computation.72 | convolution fusion | flops 301989888 | bytes 2555904 | tf_op jit(solution)/shard_map/dot_general | solution.py:59
  67.1 2.9 %fusion.74 = f32[512,768]{1,0:T(8,128)} fusion(bf16[768,5,384]{2,0,1:T(8,128)(2,1)} %param.8, bf16[516,384]{1,0:T(8,128)(2,1)S(1)} %reshape.42), kind=kOutput, calls=%fused_computation.78 | convolution fusion | flops 301989888 | bytes 2555904 | tf_op jit(solution)/shard_map/dot_general | solution.py:59
  70.0 0.9 broadcast_in_dim.20
  71.0 1.1 slice.177
  72.1 4.1 %add_convert_fusion = bf16[512,768]{1,0:T(8,128)(2,1)} fusion(f32[512,768]{1,0:T(8,128)} %fusion.68, f32[512,768]{1,0:T(8,128)S(1)} %fusion.71, f32[512,768]{1,0:T(8,128)} %fusion.77, f32[512,768]{1,0:T(8,128)} %fusion.74, bf16[512,384]{1,0:T(8,128)(2,1)S(1)} %slice.177, bf16[768,5,384]{2,0,1:T(8,128)(2,1)} %param.8), kind=kOutput, calls=%fused_computation.20 | convolution fusion | flops 303955968 | bytes 8060928 | tf_op jit(solution)/shard_map/dot_general | solution.py:59
  76.2 1.5 copy.33
  77.7 1.3 copy.34
  79.1 60.2 %shard_map.78 = (bf16[512,192]{1,0:T(8,128)(2,1)S(1)}, bf16[4,544,192]{2,1,0:T(8,128)(2,1)}, bf16[4,512,192]{2,1,0:T(8,128)(2,1)S(1)}) custom-call(bf16[4,512,192]{2,1,0:T(8,128)(2,1)} %bitcast.137, bf16[512,192]{1,0:T(8,128)(2,1)S(1)} %pad_dynamic-slice_fusion.stem_ref, bf16[512,192]{1,0:T(8,128)(2,1)S(1)} %copy.35.target_ref), custom_call_target="tpu_custom_call" | custom-call | tf_op jit(solution)/shard_map/pallas_call | solution.py:349
  139.3 17.9 %all_gather.3 = bf16[1024,384]{1,0:T(8,128)(2,1)S(1)} all-gather(bf16[256,384]{1,0:T(8,128)(2,1)S(1)} %get-tuple-element.27), channel_id=1, replica_groups=mesh['groups'=2,'seq'=4,'chan'=4] {'seq'}, dimensions={0}, use_global_device_ids=true | all-gather | bytes 983040 | tf_op jit(solution)/shard_map/all_gather | solution.py:411
  157.2 2.0 broadcast_in_dim.22
  159.2 4.7 %reshape.47 = bf16[2048,384]{1,0:T(8,128)(2,1)} reshape(bf16[1024,2,384]{2,1,0:T(2,128)(2,1)} %broadcast_in_dim.22) | data formatting | bytes 3145728 | tf_op jit(solution)/shard_map/reshape | solution.py:445
  163.9 2.1 fusion.17
  169.9 1.0 copy-done.5
  174.4 0.9 reduce_sum.9
  176.7 72.4 %shard_map.79 = bf16[4,512,384]{2,1,0:T(8,128)(2,1)S(1)} custom-call(bf16[512,384]{1,0:T(8,128)(2,1)S(1)} %fusion.58.own_ref), custom_call_target="tpu_custom_call" | custom-call | tf_op jit(solution)/shard_map/pallas_call | solution.py:349
  249.7 0.6 fusion.30
  252.3 0.9 copy.36
  (50 shorter events, 12.3 us)
Async XLA Ops:
  0.6 5.5 %copy-start = (bf16[192,5,4]{0,2,1:T(4,128)(2,1)S(1)}, bf16[192,5,4]{0,2,1:T(4,128)(2,1)}, u32[]{:S(2)}) copy-start(bf16[192,5,4]{0,2,1:T(4,128)(2,1)} %param.6) | copy-start | bytes 23044
  0.6 0.7 copy-start.1
  7.1 16.6 %copy-start.3 = (bf16[2048,192]{1,0:T(8,128)(2,1)}, bf16[2048,192]{1,0:T(8,128)(2,1)S(1)}, u32[]{:S(2)}) copy-start(bf16[2048,192]{1,0:T(8,128)(2,1)S(1)} %fusion.5) | copy-start | bytes 2359300
  55.9 1.7 copy-start.8
  67.1 2.9 %copy-start.7 = (bf16[256,384]{1,0:T(8,128)(2,1)S(1)}, bf16[256,384]{1,0:T(8,128)(2,1)}, u32[]{:S(2)}) copy-start(bf16[256,384]{1,0:T(8,128)(2,1)} %get-tuple-element.26) | copy-start | bytes 589828
  76.2 2.8 %copy-start.9 = (bf16[512,192]{0,1:T(8,128)(2,1)S(1)}, bf16[512,192]{0,1:T(8,128)(2,1)}, u32[]{:S(2)}) copy-start(bf16[512,192]{0,1:T(8,128)(2,1)} %param.9) | copy-start | bytes 589828
  163.9 2.2 copy-start.2
  167.9 1.2 copy-start.6
  168.5 1.1 copy-start.10
  169.1 1.8 copy-start.5
  176.2 72.9 %copy-start.4 = (bf16[2048,192]{1,0:T(8,128)(2,1)S(1)}, bf16[2048,192]{1,0:T(8,128)(2,1)}, u32[]{:S(2)}) copy-start(bf16[2048,192]{1,0:T(8,128)(2,1)} %copy-done.3) | copy-start | bytes 2359300
  252.3 1.2 copy-start.11

commit v2 on v1

--- a/solution.py
+++ b/solution.py
@@ -125,7 +125,7 @@
 MESH_ID = pl.DeviceIdType.MESH
 BF16 = jnp.bfloat16
 EDGE = 16
-VMEM_BYTES = 52 * 1024 * 1024
+VMEM_BYTES = 8 * 1024 * 1024
 
 
 def send(src, dst, send_sem, recv_sem, seq, chan):
@@ -174,39 +174,122 @@
         copy.wait()
 
 
+def partners(c):
+    mate = c + 1 - 2 * lax.rem(c, 2)
+    across = lax.rem(c + 2, 4)
+    return mate, across, lax.rem(mate + 2, 4)
+
+
+class Turn:
+    def __init__(self, n, s, c, own, out, sems):
+        self.n, self.s, self.c, self.own, self.out = n, s, c, own, out
+        self.quarter_send, self.quarter_recv, self.share_send, self.share_recv, self.local = sems
+        self.piece = own.shape[0] // n
+
+    def rows(self, index):
+        return pl.ds(pl.multiple_of(index * self.piece, self.piece), self.piece)
+
+    def keep(self):
+        at = self.rows(self.c)
+        return pltpu.make_async_copy(self.own.at[at], self.out.at[self.s, at], self.local)
+
+    def quarter(self, q, slot):
+        at = self.rows(q)
+        return send(self.own.at[at], self.out.at[self.s, at], self.quarter_send.at[q],
+                    self.quarter_recv.at[slot], self.c, q)
+
+    def each(self, action, mine):
+        for q in range(self.n):
+            itself = jnp.logical_and(self.s == self.c, self.c == q)
+            pl.when(jnp.logical_not(itself))(functools.partial(action, q))
+        if mine is not None:
+            pl.when(self.s == self.c)(mine)
+
+    def start(self):
+        self.each(lambda q: self.quarter(q, self.s).start(), lambda: self.keep().start())
+
+    def share(self, slot, kind, part, to):
+        at = self.rows(part)
+        index = slot * 3 + kind
+        return send(self.out.at[slot, at], self.out.at[slot, at], self.share_send.at[index],
+                    self.share_recv.at[index], self.s, to)
+
+    def finish(self):
+        mate, across, far = partners(self.c)
+        slots = [lax.rem(self.s + d, self.n) for d in range(self.n)]
+        for d, slot in enumerate(slots):
+            if d == 0:
+                pl.when(self.s == self.c)(lambda: self.keep().wait())
+                pl.when(self.s != self.c)(lambda: self.quarter(self.c, slot).wait_recv())
+            else:
+                self.quarter(self.c, slot).wait_recv()
+            self.share(slot, 1, self.c, across).start()
+            self.share(slot, 0, self.c, mate).start()
+        for slot in slots:
+            self.share(slot, 1, across, across).wait_recv()
+            self.share(slot, 2, across, mate).start()
+        for slot in slots:
+            self.share(slot, 0, mate, mate).wait_recv()
+            self.share(slot, 2, far, mate).wait_recv()
+        for slot in slots:
+            self.share(slot, 0, self.c, mate).wait_send()
+            self.share(slot, 1, self.c, across).wait_send()
+            self.share(slot, 2, across, mate).wait_send()
+        self.each(lambda q: self.quarter(q, self.s).wait_send(), None)
+
+
+def pair_sum(block, held, pair, s, c, rows, send_sem, recv_sem, finish):
+    mate, across, far = partners(c)
+    first = send(block(far), held.at[1], send_sem.at[1], recv_sem.at[1], s, mate)
+    second = send(block(mate), held.at[0], send_sem.at[0], recv_sem.at[0], s, mate)
+    last = send(pair, held.at[2], send_sem.at[2], recv_sem.at[2], s, across)
+    first.start()
+    second.start()
+    step = 64
+    first.wait_recv()
+
+    @pl.loop(0, rows // step)
+    def _(i):
+        at = pl.ds(pl.multiple_of(i * step, step), step)
+        pair[at, :] = (
+            block(across)[at, :].astype(jnp.float32) + held[1, at, :].astype(jnp.float32)
+        ).astype(BF16)
+
+    last.start()
+    second.wait_recv()
+    last.wait_recv()
+
+    @pl.loop(0, rows // step)
+    def _(i):
+        at = pl.ds(pl.multiple_of(i * step, step), step)
+        total = block(c)[at, :].astype(jnp.float32) + held[0, at, :].astype(jnp.float32)
+        finish(at, total + held[2, at, :].astype(jnp.float32))
+
+    return [first, second, last]
+
+
 def encoder_kernel(
-    n, part_ref, pre_ref, pool_ref, held, wide, edge_lo, edge_hi,
+    n, part_ref, pre_ref, pool_ref, held, pair, wide, edge_lo, edge_hi,
     send_sem, recv_sem, edge_send, edge_recv,
 ):
     s, c = lax.axis_index("seq"), lax.axis_index("chan")
     rows, width = pre_ref.shape
     half = rows // 2
-    peers = [lax.rem(c + d, n) for d in range(1, n)]
-    greet([(s, p) for p in peers] + [(lax.rem(s + d, n), c) for d in range(1, n)])
-    copies = []
-    for d, p in enumerate(peers):
-        columns = pl.ds(pl.multiple_of(p * width, 128), width)
-        copies.append(
-            send(part_ref.at[:, columns], held.at[d], send_sem.at[d], recv_sem.at[d], s, p)
-        )
-    for copy in copies:
-        copy.start()
-    own = pl.ds(pl.multiple_of(c * width, 128), width)
-    for copy in copies:
-        copy.wait_recv()
-    step = 64
-
-    @pl.loop(0, rows // step)
-    def _(i):
-        at = pl.ds(pl.multiple_of(i * step, step), step)
-        total = part_ref[at, own].astype(jnp.float32)
-        for d in range(n - 1):
-            total = total + held[d, at, :].astype(jnp.float32)
+    greet(
+        [(s, lax.rem(c + d, n)) for d in range(1, n)]
+        + [(lax.rem(s + d, n), c) for d in range(1, n)]
+    )
+
+    def block(j):
+        return part_ref.at[:, pl.ds(pl.multiple_of(j * width, 128), width)]
+
+    def finish(at, total):
         pre_ref[at, :] = total
         active = gelu_value(total).astype(BF16).astype(jnp.float32)
         for j in range(width // 128):
             wide[j, at, :] = active[:, j * 128 : (j + 1) * 128]
 
+    copies = pair_sum(block, held, pair, s, c, rows, send_sem, recv_sem, finish)
     for j in range(width // 128):
         even = wide[j, pl.ds(0, half, stride=2), :]
         odd = wide[j, pl.ds(1, half, stride=2), :]
@@ -228,40 +311,41 @@
 
 
 def slope_kernel(
-    n, scale, part_ref, stem_ref, target_ref, pred_ref, chan_ref, seq_ref, held, slope,
-    send_sem, recv_sem, row_send, row_recv, turn_send, turn_recv, lo_send, lo_recv, hi_send, hi_recv,
-    local_sem,
+    n, scale, part_ref, stem_ref, target_ref, pool_ref, pred_ref, chan_ref, seq_ref, all_ref,
+    held, pair, slope, send_sem, recv_sem, row_send, row_recv, lo_send, lo_recv, hi_send, hi_recv,
+    pool_send, pool_recv, local_sem, *turn_sems,
 ):
     s, c = lax.axis_index("seq"), lax.axis_index("chan")
     rows, width = pred_ref.shape
-    peers = [lax.rem(c + d, n) for d in range(1, n)]
+    mate, across, far = partners(c)
     greet(whole_group(n, s, c))
-    copies = [
-        send(part_ref.at[p], held.at[d], send_sem.at[d], recv_sem.at[d], s, p)
-        for d, p in enumerate(peers)
-    ]
-    for copy in copies:
-        copy.start()
-    for copy in copies:
-        copy.wait_recv()
-    step = 64
-
-    @pl.loop(0, rows // step)
-    def _(i):
-        at = pl.ds(pl.multiple_of(i * step, step), step)
-        total = part_ref[c, at, :].astype(jnp.float32)
-        for d in range(n - 1):
-            total = total + held[d, at, :].astype(jnp.float32)
+    pool_own = pool_ref.at[pl.ds(EDGE, rows // 2)]
+
+    def finish(at, total):
         output = total + stem_ref[at, :].astype(jnp.float32)
         pred_ref[at, :] = output.astype(BF16)
         slope[at, :] = ((output - target_ref[at, :].astype(jnp.float32)) * scale).astype(BF16)
 
+    pool_copies = [
+        send(pool_own, all_ref.at[s], pool_send.at[d], pool_recv.at[d], lax.rem(s + 1 + d, n), c)
+        for d in range(n - 1)
+    ]
+    pool_mine = pltpu.make_async_copy(pool_own, all_ref.at[s], local_sem.at[1])
+    for copy in pool_copies:
+        copy.start()
+    pool_mine.start()
+    copies = pair_sum(
+        lambda j: part_ref.at[j], held, pair, s, c, rows, send_sem, recv_sem, finish
+    )
     core = pl.ds(EDGE, rows)
     up, down = lax.rem(s + 1, n), lax.rem(s + n - 1, n)
-    row_copies = [
-        send(slope, chan_ref.at[c, core], row_send.at[d], row_recv.at[d], s, p)
-        for d, p in enumerate(peers)
-    ]
+
+    def row_copy(index, src, owner, to):
+        return send(src, chan_ref.at[owner, core], row_send.at[index], row_recv.at[index], s, to)
+
+    to_across = row_copy(1, slope, c, across)
+    to_mate = row_copy(0, slope, c, mate)
+    relay = row_copy(2, chan_ref.at[across, core], across, mate)
     lo_copies, hi_copies = [], []
     for d in range(n):
         p = lax.rem(c + d, n)
@@ -273,35 +357,22 @@
             send(slope.at[pl.ds(0, EDGE)], chan_ref.at[c, pl.ds(EDGE + rows, EDGE)],
                  hi_send.at[d], hi_recv.at[d], down, p)
         )
-    for copy in row_copies + lo_copies + hi_copies:
+    for copy in [to_across, to_mate] + lo_copies + hi_copies:
         copy.start()
     mine = pltpu.make_async_copy(slope, chan_ref.at[c, core], local_sem.at[0])
     mine.start()
-    for j in range(n):
-        turned = send(slope, seq_ref.at[s], turn_send.at[j], turn_recv.at[s], c, j)
-        itself = jnp.logical_and(s == c, c == j)
-
-        @pl.when(jnp.logical_not(itself))
-        def _():
-            turned.start()
-
-        @pl.when(itself)
-        def _():
-            keep = pltpu.make_async_copy(slope, seq_ref.at[s], local_sem.at[1])
-            keep.start()
-            keep.wait()
-
-    for copy in row_copies + lo_copies + hi_copies:
+    turn = Turn(n, s, c, slope, seq_ref, turn_sems)
+    turn.start()
+    to_across.wait_recv()
+    relay.start()
+    turn.finish()
+    to_across.wait_send()
+    to_mate.wait()
+    relay.wait()
+    for copy in lo_copies + hi_copies + pool_copies:
         copy.wait()
     mine.wait()
-    for j in range(n):
-        @pl.when(jnp.logical_not(jnp.logical_and(s == c, c == j)))
-        def _():
-            send(slope, seq_ref.at[s], turn_send.at[j], turn_recv.at[s], c, j).wait_send()
-
-        @pl.when(jnp.logical_not(jnp.logical_and(s == c, s == j)))
-        def _():
-            send(slope, seq_ref.at[j], turn_send.at[j], turn_recv.at[j], c, j).wait_recv()
+    pool_mine.wait()
     for copy in copies:
         copy.wait_send()
     blank = jnp.zeros((EDGE, width), BF16)
@@ -317,31 +388,16 @@
             chan_ref[j, EDGE + rows :, :] = blank
 
 
-def turn_kernel(n, own_ref, seq_ref, turn_send, turn_recv, local_sem):
+def turn_kernel(n, own_ref, seq_ref, *turn_sems):
     s, c = lax.axis_index("seq"), lax.axis_index("chan")
     greet(whole_group(n, s, c))
-    for j in range(n):
-        turned = send(own_ref, seq_ref.at[s], turn_send.at[j], turn_recv.at[s], c, j)
-        itself = jnp.logical_and(s == c, c == j)
-
-        @pl.when(jnp.logical_not(itself))
-        def _():
-            turned.start()
-
-        @pl.when(itself)
-        def _():
-            keep = pltpu.make_async_copy(own_ref, seq_ref.at[s], local_sem)
-            keep.start()
-            keep.wait()
-
-    for j in range(n):
-        @pl.when(jnp.logical_not(jnp.logical_and(s == c, c == j)))
-        def _():
-            send(own_ref, seq_ref.at[s], turn_send.at[j], turn_recv.at[s], c, j).wait_send()
-
-        @pl.when(jnp.logical_not(jnp.logical_and(s == c, s == j)))
-        def _():
-            send(own_ref, seq_ref.at[j], turn_send.at[j], turn_recv.at[j], c, j).wait_recv()
+    turn = Turn(n, s, c, own_ref, seq_ref, turn_sems)
+    turn.start()
+    turn.finish()
+
+
+def turn_scratch(n):
+    return [dma(n), dma(n), dma(3 * n), dma(3 * n), pltpu.SemaphoreType.DMA]
 
 
 def call(kernel, ident, outs, scratch, *operands):
@@ -400,6 +456,7 @@
         (struct((rows, c2), jnp.float32), struct((rows // 2 + 2 * EDGE, c2), BF16)),
         [
             pltpu.VMEM((n - 1, rows, c2), BF16),
+            pltpu.VMEM((rows, c2), BF16),
             pltpu.VMEM((c2 // 128, rows, 128), jnp.float32),
             pltpu.VMEM((EDGE, c2), BF16),
             pltpu.VMEM((EDGE, c2), BF16),
@@ -408,24 +465,26 @@
         part,
     )
     half = rows // 2
-    pool_all = lax.all_gather(pool_pad[EDGE : EDGE + half], "seq", axis=0, tiled=True)
     up_pad = jnp.repeat(pool_pad[EDGE - 1 : EDGE + half + 1], 2, axis=0)
     dec_part = conv_rows(up_pad, w_dec).astype(BF16)
     dec_part = dec_part.reshape(rows, n, c1).transpose(1, 0, 2)
-    pred, slope_chan, slope_seq = call(
+    pred, slope_chan, slope_seq, pool_all = call(
         functools.partial(slope_kernel, n, 1.0 / math.sqrt(length)), 2,
         (
             struct((rows, c1), BF16),
             struct((n, rows + 2 * EDGE, c1), BF16),
             struct((n, rows, c1), BF16),
+            struct((n, half, c2), BF16),
         ),
         [
             pltpu.VMEM((n - 1, rows, c1), BF16),
             pltpu.VMEM((rows, c1), BF16),
-            dma(n - 1), dma(n - 1), dma(n - 1), dma(n - 1), dma(n), dma(n),
-            dma(n), dma(n), dma(n), dma(n), dma(2),
+            pltpu.VMEM((rows, c1), BF16),
+            dma(3), dma(3), dma(3), dma(3), dma(n), dma(n), dma(n), dma(n),
+            dma(n - 1), dma(n - 1), dma(2),
+            *turn_scratch(n),
         ],
-        dec_part, stem_pad[2 : 2 + rows], targets,
+        dec_part, stem_pad[2 : 2 + rows], targets, pool_pad,
     )
     slope_pad = jnp.concatenate(
         [slope_chan[j, EDGE - 2 : EDGE + rows + 2] for j in range(n)], axis=1
@@ -440,9 +499,9 @@
     pre_grad = (act_grad * gelu_slope(enc_pre)).astype(BF16)
     pre_seq = call(
         functools.partial(turn_kernel, n), 3, struct((n, rows, c2), BF16),
-        [dma(n), dma(n), pltpu.SemaphoreType.DMA], pre_grad,
-    )
-    up_all = jnp.pad(jnp.repeat(pool_all, 2, axis=0), ((2, 2), (0, 0)))
+        turn_scratch(n), pre_grad,
+    )
+    up_all = jnp.pad(jnp.repeat(pool_all.reshape(length // 2, c2), 2, axis=0), ((2, 2), (0, 0)))
     g_dec = all_rows_grad(slope_seq.reshape(length, c1), up_all)
     g_enc = all_rows_grad(pre_seq.reshape(length, c2), stem_all)
     return (pred, g_enc, g_dec)
@@ -452,7 +511,7 @@
     args = (dna_bases, w_stem, w_enc, w_dec, targets)
     rows, c1, c2 = dna_bases.shape[0], w_stem.shape[0], w_dec.shape[2]
     n = lax.axis_size("seq")
-    square = n == lax.axis_size("chan") and n > 2
+    square = n == 4 and lax.axis_size("chan") == 4
     if square and rows % 128 == 0 and c2 % 128 == 0 and c1 % 64 == 0:
         return square_shards(*args)
     return general_shards(*args)

time: 254 us -> 159 us (0.63)
  the two profiles are of different devices: /device:TPU:3 before, /device:TPU:0 now
where the time goes in v2:
time: 159 us
  Pallas kernels  94.5 us (59%)
  matrix products  43.5 us (27%)
  local copies, waits for them, and re-layouts  17.8 us (11%)
  other arithmetic  1.79 us (1%)
    pallas_call x4, Pallas kernels, call(): pl.pallas_call(kernel, out_shape=outs, in_specs=[vmem] * len(operands), o...  94.5 us
    dot_general x10, matrix products, conv_rows(): lax.dot_general(padded[k:k + row_count], weight[:, k, :], (((1,), (1,)),...  33.5 us
    dot_general x10, matrix products, all_rows_grad(): lax.dot_general(cotangent, padded[k:k + count], (((0,), (0,)), ((), ())),...  6.13 us
    unnamed x28, local copies, waits for them, and re-layouts  5.67 us
    reshape x1, local copies, waits for them, and re-layouts, square_shards(): jnp.repeat(pool_all.reshape(length // 2, c2), 2, axis=0)  3.67 us

profile of v2, /device:TPU:0, one launch (start us, length us, event | category | flops | bytes accessed | tf_op | source)
XLA Modules:
  0.0 158.7 jit_solution(3532539040585523357)
XLA Ops:
  0.7 0.7 copy-done.5
  1.3 7.3 %shard_map.76 = s32[4,4,128]{2,1,0:T(4,128)S(1)} custom-call(s32[4,128]{1,0:T(4,128)S(1)} %bitcast.139), custom_call_target="tpu_custom_call" | custom-call | tf_op jit(solution)/shard_map/pallas_call | solution.py:405
  8.8 0.9 fusion.5
  9.7 3.7 %fusion.83 = f32[512,1536]{1,0:T(8,128)} fusion(bf16[1536,5,192]{0,2,1:T(8,128)(2,1)} %param.7, s32[]{:T(128)S(6)} %select_n.3, bf16[2048,192]{1,0:T(8,128)(2,1)S(1)} %fusion.5), kind=kOutput, calls=%fused_computation.87 | convolution fusion | flops 301989888 | bytes 4521988 | tf_op jit(solution)/shard_map/dot_general | solution.py:59
  13.4 4.3 %convolution_add_fusion.3 = f32[512,1536]{1,0:T(8,128)} fusion(f32[512,1536]{1,0:T(8,128)} %fusion.83, bf16[1536,5,192]{0,2,1:T(8,128)(2,1)} %param.7, s32[]{:T(128)S(6)} %add.86, bf16[2048,192]{1,0:T(8,128)(2,1)S(1)} %fusion.5), kind=kOutput, calls=%fused_computation.3 | convolution fusion | flops 302776320 | bytes 7667716 | tf_op jit(solution)/shard_map/dot_general | solution.py:59
  17.7 4.3 %convolution_add_fusion.2 = f32[512,1536]{1,0:T(8,128)} fusion(f32[512,1536]{1,0:T(8,128)} %convolution_add_fusion.3, bf16[512,192]{1,0:T(8,128)(2,1)S(1)} %pad_dynamic-slice_fusion.stem_ref, bf16[1536,5,192]{0,2,1:T(8,128)(2,1)} %param.7), kind=kOutput, calls=%fused_computation.2 | convolution fusion | flops 302776320 | bytes 7077888 | tf_op jit(solution)/shard_map/dot_general | solution.py:59
  22.1 4.3 %convolution_add_fusion.1 = f32[512,1536]{1,0:T(8,128)} fusion(f32[512,1536]{1,0:T(8,128)} %convolution_add_fusion.2, bf16[1536,5,192]{0,2,1:T(8,128)(2,1)} %param.7, s32[]{:T(128)S(6)} %add.88, bf16[2048,192]{1,0:T(8,128)(2,1)S(1)} %fusion.5), kind=kOutput, calls=%fused_computation.1 | convolution fusion | flops 302776320 | bytes 7667716 | tf_op jit(solution)/shard_map/dot_general | solution.py:59
  26.4 2.7 %fusion.part_ref = bf16[512,1536]{1,0:T(8,128)(2,1)S(1)} fusion(f32[512,1536]{1,0:T(8,128)} %convolution_add_fusion.1, bf16[1536,5,192]{0,2,1:T(8,128)(2,1)} %param.7, s32[]{:T(128)S(6)} %add.89, bf16[2048,192]{1,0:T(8,128)(2,1)S(1)} %fusion.5), kind=kOutput, calls=%fused_computation.5 | convolution fusion | flops 303562752 | bytes 6094852 | tf_op jit(solution)/shard_map/dot_general | solution.py:59
  29.0 18.8 %shard_map.77 = (f32[512,384]{1,0:T(8,128)S(1)}, bf16[288,384]{1,0:T(8,128)(2,1)S(1)}) custom-call(bf16[512,1536]{1,0:T(8,128)(2,1)S(1)} %fusion.part_ref), custom_call_target="tpu_custom_call" | custom-call | tf_op jit(solution)/shard_map/pallas_call | solution.py:405
  47.9 0.9 fusion.132
  49.1 1.7 %fusion.71 = f32[512,768]{1,0:T(8,128)S(1)} fusion(bf16[512,384]{1,0:T(8,128)(2,1)S(1)} %slice.171, bf16[768,5,384]{2,0,1:T(8,128)(2,1)} %param.8), kind=kOutput, calls=%fused_computation.75 | convolution fusion | flops 301989888 | bytes 2555904 | tf_op jit(solution)/shard_map/dot_general | solution.py:59
  51.2 2.8 %fusion.77 = f32[512,768]{1,0:T(8,128)} fusion(bf16[512,384]{1,0:T(8,128)(2,1)S(1)} %slice.165, bf16[768,5,384]{2,0,1:T(8,128)(2,1)} %param.8), kind=kOutput, calls=%fused_computation.81 | convolution fusion | flops 301989888 | bytes 2555904 | tf_op jit(solution)/shard_map/dot_general | solution.py:59
  54.9 2.9 %fusion.68 = f32[512,768]{1,0:T(8,128)} fusion(bf16[768,5,384]{2,0,1:T(8,128)(2,1)} %param.8, bf16[516,384]{1,0:T(8,128)(2,1)S(1)} %reshape.45), kind=kOutput, calls=%fused_computation.72 | convolution fusion | flops 301989888 | bytes 2555904 | tf_op jit(solution)/shard_map/dot_general | solution.py:59
  57.8 2.8 %fusion.74 = f32[512,768]{1,0:T(8,128)} fusion(bf16[768,5,384]{2,0,1:T(8,128)(2,1)} %param.8, bf16[516,384]{1,0:T(8,128)(2,1)S(1)} %reshape.45), kind=kOutput, calls=%fused_computation.78 | convolution fusion | flops 301989888 | bytes 2555904 | tf_op jit(solution)/shard_map/dot_general | solution.py:59
  61.0 4.1 %add_convert_fusion = bf16[512,768]{1,0:T(8,128)(2,1)} fusion(f32[512,768]{1,0:T(8,128)} %fusion.68, f32[512,768]{1,0:T(8,128)S(1)} %fusion.71, f32[512,768]{1,0:T(8,128)} %fusion.77, f32[512,768]{1,0:T(8,128)} %fusion.74, bf16[512,384]{1,0:T(8,128)(2,1)S(1)} %slice.176, bf16[768,5,384]{2,0,1:T(8,128)(2,1)} %param.8), kind=kOutput, calls=%fused_computation.20 | convolution fusion | flops 303955968 | bytes 8060928 | tf_op jit(solution)/shard_map/dot_general | solution.py:59
  65.1 1.5 copy.33
  67.2 41.0 %shard_map.78 = (bf16[512,192]{1,0:T(8,128)(2,1)S(1)}, bf16[4,544,192]{2,1,0:T(8,128)(2,1)S(1)}, bf16[4,512,192]{2,1,0:T(8,128)(2,1)S(1)}, bf16[4,256,384]{2,1,0:T(8,128)(2,1)S(1)}) custom-call(bf16[4,512,192]{2,1,0:T(8,128)(2,1)S(1)} %bitcast.130, bf16[512,192]{1,0:T(8,128)(2,1)S(1)} %pad_dynamic-slice_fusion.stem_ref, ...), custom_call_target="tpu_custom_call" | custom-call | tf_op jit(solution)/shard_map/pallas_call | solution.py:405
  108.2 1.0 copy-done.1
  109.2 2.0 %broadcast_in_dim.22 = bf16[1024,2,384]{2,1,0:T(2,128)(2,1)} broadcast(bf16[1024,384]{1,0:T(8,128)(2,1)S(1)} %bitcast.136), dimensions={0,2} | broadcast | bytes 2359296 | tf_op jit(solution)/shard_map/broadcast_in_dim | solution.py:504
  111.2 3.7 %reshape.51 = bf16[2048,384]{1,0:T(8,128)(2,1)S(1)} reshape(bf16[1024,2,384]{2,1,0:T(2,128)(2,1)} %broadcast_in_dim.22) | data formatting | bytes 3145728 | tf_op jit(solution)/shard_map/reshape | solution.py:504
  114.9 0.6 fusion.17
  116.1 0.6 fusion.26
  118.0 1.1 copy-done.11
  119.6 1.3 copy-done.8
  124.3 0.9 reduce_sum.9
  126.9 27.4 %shard_map.79 = bf16[4,512,384]{2,1,0:T(8,128)(2,1)S(1)} custom-call(bf16[512,384]{1,0:T(8,128)(2,1)S(1)} %fusion.58.own_ref), custom_call_target="tpu_custom_call" | custom-call | tf_op jit(solution)/shard_map/pallas_call | solution.py:405
  154.4 0.6 fusion.31
  155.0 0.6 fusion.30
  155.6 0.6 fusion.29
  156.2 0.6 fusion.28
  156.9 0.6 fusion.27
  157.5 1.0 copy.36
  (51 shorter events, 10.4 us)
Async XLA Ops:
  0.6 8.1 %copy-start = (bf16[192,5,4]{0,2,1:T(4,128)(2,1)S(1)}, bf16[192,5,4]{0,2,1:T(4,128)(2,1)}, u32[]{:S(2)}) copy-start(bf16[192,5,4]{0,2,1:T(4,128)(2,1)} %param.6) | copy-start | bytes 23044
  0.6 0.7 copy-start.5
  9.7 16.7 %copy-start.6 = (bf16[2048,192]{1,0:T(8,128)(2,1)}, bf16[2048,192]{1,0:T(8,128)(2,1)S(1)}, u32[]{:S(2)}) copy-start(bf16[2048,192]{1,0:T(8,128)(2,1)S(1)} %fusion.5) | copy-start | bytes 2359300
  47.9 3.0 %copy-start.3 = (f32[512,384]{1,0:T(8,128)}, f32[512,384]{1,0:T(8,128)S(1)}, u32[]{:S(2)}) copy-start(f32[512,384]{1,0:T(8,128)S(1)} %get-tuple-element.12) | copy-start | bytes 2359300
  49.1 1.7 %copy-start.9 = (bf16[256,384]{1,0:T(8,128)(2,1)S(1)}, bf16[256,384]{1,0:T(8,128)(2,1)}, u32[]{:S(2)}) copy-start(bf16[256,384]{1,0:T(8,128)(2,1)} %get-tuple-element.30) | copy-start | bytes 589828
  65.1 2.0 %copy-start.10 = (bf16[512,192]{0,1:T(8,128)(2,1)S(1)}, bf16[512,192]{0,1:T(8,128)(2,1)}, u32[]{:S(2)}) copy-start(bf16[512,192]{0,1:T(8,128)(2,1)} %param.9) | copy-start | bytes 589828
  108.2 1.0 copy-start.1
  117.3 1.7 %copy-start.2 = (bf16[4,544,192]{2,1,0:T(8,128)(2,1)S(1)}, bf16[4,544,192]{2,1,0:T(8,128)(2,1)}, u32[]{:S(2)}) copy-start(bf16[4,544,192]{2,1,0:T(8,128)(2,1)} %copy-done.1) | copy-start | bytes 2506756
  117.9 1.1 copy-start.11
  119.1 1.8 %copy-start.8 = (bf16[768,5,384]{2,0,1:T(8,128)(2,1)S(1)}, bf16[768,5,384]{2,0,1:T(8,128)(2,1)}, u32[]{:S(2)}) copy-start(bf16[768,5,384]{2,0,1:T(8,128)(2,1)} %param.8) | copy-start | bytes 8847364
  125.3 1.1 copy-start.4
  126.4 27.9 %copy-start.7 = (bf16[2048,192]{1,0:T(8,128)(2,1)S(1)}, bf16[2048,192]{1,0:T(8,128)(2,1)}, u32[]{:S(2)}) copy-start(bf16[2048,192]{1,0:T(8,128)(2,1)} %copy-done.6) | copy-start | bytes 2359300
  157.5 1.2 copy-start.12

commit v3 on v2

--- a/solution.py
+++ b/solution.py
@@ -198,15 +198,19 @@
         return send(self.own.at[at], self.out.at[self.s, at], self.quarter_send.at[q],
                     self.quarter_recv.at[slot], self.c, q)
 
-    def each(self, action, mine):
+    def each(self, action, mine, before=None):
         for q in range(self.n):
+            if before is not None:
+                before(q * self.piece)
             itself = jnp.logical_and(self.s == self.c, self.c == q)
             pl.when(jnp.logical_not(itself))(functools.partial(action, q))
         if mine is not None:
             pl.when(self.s == self.c)(mine)
 
-    def start(self):
-        self.each(lambda q: self.quarter(q, self.s).start(), lambda: self.keep().start())
+    def start(self, before=None):
+        self.each(
+            lambda q: self.quarter(q, self.s).start(), lambda: self.keep().start(), before
+        )
 
     def share(self, slot, kind, part, to):
         at = self.rows(part)
@@ -214,7 +218,7 @@
         return send(self.out.at[slot, at], self.out.at[slot, at], self.share_send.at[index],
                     self.share_recv.at[index], self.s, to)
 
-    def finish(self):
+    def finish(self, between=None):
         mate, across, far = partners(self.c)
         slots = [lax.rem(self.s + d, self.n) for d in range(self.n)]
         for d, slot in enumerate(slots):
@@ -225,6 +229,8 @@
                 self.quarter(self.c, slot).wait_recv()
             self.share(slot, 1, self.c, across).start()
             self.share(slot, 0, self.c, mate).start()
+        if between is not None:
+            between()
         for slot in slots:
             self.share(slot, 1, across, across).wait_recv()
             self.share(slot, 2, across, mate).start()
@@ -268,8 +274,17 @@
     return [first, second, last]
 
 
+def pair_add(value):
+    count = value.shape[0]
+    row = lax.broadcasted_iota(jnp.int32, value.shape, 0)
+    other = jnp.where(
+        lax.rem(row, 2) == 0, pltpu.roll(value, count - 1, 0), pltpu.roll(value, 1, 0)
+    )
+    return value + other
+
+
 def encoder_kernel(
-    n, part_ref, pre_ref, pool_ref, held, pair, wide, edge_lo, edge_hi,
+    n, part_ref, pre_ref, up_ref, pool_ref, held, pair, wide,
     send_sem, recv_sem, edge_send, edge_recv,
 ):
     s, c = lax.axis_index("seq"), lax.axis_index("chan")
@@ -286,57 +301,99 @@
     def finish(at, total):
         pre_ref[at, :] = total
         active = gelu_value(total).astype(BF16).astype(jnp.float32)
+        pooled = (0.5 * pair_add(active)).astype(BF16)
+        up_ref[pl.ds(pl.multiple_of(at.start + EDGE, EDGE), at.size), :] = pooled
         for j in range(width // 128):
-            wide[j, at, :] = active[:, j * 128 : (j + 1) * 128]
+            wide[j, at, :] = pooled[:, j * 128 : (j + 1) * 128].astype(jnp.float32)
 
     copies = pair_sum(block, held, pair, s, c, rows, send_sem, recv_sem, finish)
-    for j in range(width // 128):
-        even = wide[j, pl.ds(0, half, stride=2), :]
-        odd = wide[j, pl.ds(1, half, stride=2), :]
-        pool_ref[EDGE : EDGE + half, j * 128 : (j + 1) * 128] = (0.5 * (even + odd)).astype(BF16)
-    up = send(pool_ref.at[pl.ds(half, EDGE)], edge_lo, edge_send.at[0], edge_recv.at[0],
-              lax.rem(s + 1, n), c)
-    down = send(pool_ref.at[pl.ds(EDGE, EDGE)], edge_hi, edge_send.at[1], edge_recv.at[1],
-                lax.rem(s + n - 1, n), c)
+    up = send(up_ref.at[pl.ds(rows, EDGE)], up_ref.at[pl.ds(0, EDGE)], edge_send.at[0],
+              edge_recv.at[0], lax.rem(s + 1, n), c)
+    down = send(up_ref.at[pl.ds(EDGE, EDGE)], up_ref.at[pl.ds(rows + EDGE, EDGE)],
+                edge_send.at[1], edge_recv.at[1], lax.rem(s + n - 1, n), c)
     up.start()
     down.start()
+    for j in range(width // 128):
+        pool_ref[:, j * 128 : (j + 1) * 128] = wide[j, pl.ds(0, half, stride=2), :].astype(BF16)
     up.wait()
     down.wait()
-    pool_ref[0:EDGE, :] = jnp.where(s > 0, edge_lo[...].astype(jnp.float32), 0.0).astype(BF16)
-    pool_ref[half + EDGE :, :] = jnp.where(
-        s < n - 1, edge_hi[...].astype(jnp.float32), 0.0
-    ).astype(BF16)
+    blank = jnp.zeros((EDGE, width), BF16)
+
+    @pl.when(s == 0)
+    def _():
+        up_ref[0:EDGE, :] = blank
+
+    @pl.when(s == n - 1)
+    def _():
+        up_ref[rows + EDGE :, :] = blank
+
     for copy in copies:
         copy.wait_send()
 
 
+class PoolRelay:
+    def __init__(self, n, s, c, own, out, right_send, left_send, recv, local):
+        self.n, self.s, self.c, self.own, self.out = n, s, c, own, out
+        self.right_send, self.left_send, self.recv = right_send, left_send, recv
+        self.mine = pltpu.make_async_copy(own, out.at[s], local)
+
+    def hop(self, src, slot, step):
+        sems = self.right_send if step > 0 else self.left_send
+        return send(src, self.out.at[slot], sems.at[slot], self.recv.at[slot], self.s + step, self.c)
+
+    def start(self):
+        pl.when(self.s < self.n - 1)(lambda: self.hop(self.own, self.s, 1).start())
+        pl.when(self.s > 0)(lambda: self.hop(self.own, self.s, -1).start())
+        self.mine.start()
+
+    def arrive(self, d):
+        low, high = self.s - d, self.s + d
+
+        @pl.when(low >= 0)
+        def _():
+            self.hop(self.out.at[low], low, 1).wait_recv()
+            pl.when(self.s < self.n - 1)(lambda: self.hop(self.out.at[low], low, 1).start())
+
+        @pl.when(high < self.n)
+        def _():
+            self.hop(self.out.at[high], high, -1).wait_recv()
+            pl.when(self.s > 0)(lambda: self.hop(self.out.at[high], high, -1).start())
+
+    def end(self):
+        self.mine.wait()
+        for slot in range(self.n):
+            pl.when(jnp.logical_and(slot <= self.s, self.s < self.n - 1))(
+                lambda: self.hop(self.own, slot, 1).wait_send()
+            )
+            pl.when(jnp.logical_and(slot >= self.s, self.s > 0))(
+                lambda: self.hop(self.own, slot, -1).wait_send()
+            )
+
+
 def slope_kernel(
-    n, scale, part_ref, stem_ref, target_ref, pool_ref, pred_ref, chan_ref, seq_ref, all_ref,
-    held, pair, slope, send_sem, recv_sem, row_send, row_recv, lo_send, lo_recv, hi_send, hi_recv,
-    pool_send, pool_recv, local_sem, *turn_sems,
+    n, scale, part_ref, stem_ref, target_ref, pool_ref, pred_ref, chan_ref, seq_ref, up_ref,
+    held, pair, slope, all_ref, wide, send_sem, recv_sem, row_send, row_recv, lo_send, lo_recv, hi_send, hi_recv,
+    right_send, left_send, pool_recv, local_sem, *turn_sems,
 ):
     s, c = lax.axis_index("seq"), lax.axis_index("chan")
     rows, width = pred_ref.shape
     mate, across, far = partners(c)
     greet(whole_group(n, s, c))
-    pool_own = pool_ref.at[pl.ds(EDGE, rows // 2)]
+    half, up_width = pool_ref.shape
+    pools = PoolRelay(
+        n, s, c, pool_ref, all_ref, right_send, left_send, pool_recv, local_sem.at[1]
+    )
 
     def finish(at, total):
         output = total + stem_ref[at, :].astype(jnp.float32)
         pred_ref[at, :] = output.astype(BF16)
         slope[at, :] = ((output - target_ref[at, :].astype(jnp.float32)) * scale).astype(BF16)
 
-    pool_copies = [
-        send(pool_own, all_ref.at[s], pool_send.at[d], pool_recv.at[d], lax.rem(s + 1 + d, n), c)
-        for d in range(n - 1)
-    ]
-    pool_mine = pltpu.make_async_copy(pool_own, all_ref.at[s], local_sem.at[1])
-    for copy in pool_copies:
-        copy.start()
-    pool_mine.start()
+    pools.start()
     copies = pair_sum(
         lambda j: part_ref.at[j], held, pair, s, c, rows, send_sem, recv_sem, finish
     )
+    pools.arrive(1)
     core = pl.ds(EDGE, rows)
     up, down = lax.rem(s + 1, n), lax.rem(s + n - 1, n)
 
@@ -363,16 +420,30 @@
     mine.start()
     turn = Turn(n, s, c, slope, seq_ref, turn_sems)
     turn.start()
+    pools.arrive(2)
     to_across.wait_recv()
     relay.start()
-    turn.finish()
+
+    def upsample():
+        pools.arrive(3)
+        pools.end()
+
+        @pl.loop(0, n)
+        def _(slot):
+            for j in range(up_width // 128):
+                lanes = slice(j * 128, (j + 1) * 128)
+                value = all_ref[slot, :, lanes].astype(jnp.float32)
+                wide[j, pl.ds(0, half, stride=2), :] = value
+                wide[j, pl.ds(1, half, stride=2), :] = value
+                up_ref[slot, :, lanes] = wide[j].astype(BF16)
+
+    turn.finish(upsample)
     to_across.wait_send()
     to_mate.wait()
     relay.wait()
-    for copy in lo_copies + hi_copies + pool_copies:
+    for copy in lo_copies + hi_copies:
         copy.wait()
     mine.wait()
-    pool_mine.wait()
     for copy in copies:
         copy.wait_send()
     blank = jnp.zeros((EDGE, width), BF16)
@@ -388,11 +459,21 @@
             chan_ref[j, EDGE + rows :, :] = blank
 
 
-def turn_kernel(n, own_ref, seq_ref, *turn_sems):
+def turn_kernel(n, grad_ref, pre_ref, seq_ref, own, *turn_sems):
     s, c = lax.axis_index("seq"), lax.axis_index("chan")
     greet(whole_group(n, s, c))
-    turn = Turn(n, s, c, own_ref, seq_ref, turn_sems)
-    turn.start()
+    turn = Turn(n, s, c, own, seq_ref, turn_sems)
+    step = 64
+    pieces = turn.piece // step
+
+    def slope_rows(first):
+        @pl.loop(0, pieces)
+        def _(i):
+            at = pl.ds(pl.multiple_of(first + i * step, step), step)
+            grad = 0.5 * pair_add(grad_ref[at, :])
+            own[at, :] = (grad * gelu_slope(pre_ref[at, :])).astype(BF16)
+
+    turn.start(slope_rows)
     turn.finish()
 
 
@@ -416,6 +497,17 @@
 
 def dma(count):
     return pltpu.SemaphoreType.DMA((count,))
+
+
+def windows(padded):
+    count = padded.shape[0] - 4
+    return jnp.stack([padded[k : k + count] for k in range(KW)], axis=0)
+
+
+def conv_stack(padded, weight):
+    return lax.dot_general(
+        windows(padded), weight, (((0, 2), (1, 2)), ((), ())), preferred_element_type=jnp.float32
+    )
 
 
 def all_rows_grad(cotangent, padded):
@@ -450,58 +542,58 @@
     )
     stem_all = jnp.pad(gelu_value(stem_pre).astype(BF16), ((2, 2), (0, 0)))
     stem_pad = lax.dynamic_slice_in_dim(stem_all, s * rows, rows + 4, 0)
-    part = conv_rows(stem_pad, w_enc).astype(BF16)
-    enc_pre, pool_pad = call(
+    part = conv_stack(stem_pad, w_enc).astype(BF16)
+    half = rows // 2
+    enc_pre, up_own, pool = call(
         functools.partial(encoder_kernel, n), 1,
-        (struct((rows, c2), jnp.float32), struct((rows // 2 + 2 * EDGE, c2), BF16)),
+        (
+            struct((rows, c2), jnp.float32),
+            struct((rows + 2 * EDGE, c2), BF16),
+            struct((half, c2), BF16),
+        ),
         [
             pltpu.VMEM((n - 1, rows, c2), BF16),
             pltpu.VMEM((rows, c2), BF16),
             pltpu.VMEM((c2 // 128, rows, 128), jnp.float32),
-            pltpu.VMEM((EDGE, c2), BF16),
-            pltpu.VMEM((EDGE, c2), BF16),
-            dma(n - 1), dma(n - 1), dma(2), dma(2),
+            dma(3), dma(3), dma(2), dma(2),
         ],
         part,
     )
-    half = rows // 2
-    up_pad = jnp.repeat(pool_pad[EDGE - 1 : EDGE + half + 1], 2, axis=0)
-    dec_part = conv_rows(up_pad, w_dec).astype(BF16)
+    up_pad = up_own[EDGE - 2 : EDGE + rows + 2]
+    dec_part = conv_stack(up_pad, w_dec).astype(BF16)
     dec_part = dec_part.reshape(rows, n, c1).transpose(1, 0, 2)
-    pred, slope_chan, slope_seq, pool_all = call(
+    pred, slope_chan, slope_seq, up_all = call(
         functools.partial(slope_kernel, n, 1.0 / math.sqrt(length)), 2,
         (
             struct((rows, c1), BF16),
             struct((n, rows + 2 * EDGE, c1), BF16),
             struct((n, rows, c1), BF16),
-            struct((n, half, c2), BF16),
+            struct((n, rows, c2), BF16),
         ),
         [
             pltpu.VMEM((n - 1, rows, c1), BF16),
             pltpu.VMEM((rows, c1), BF16),
             pltpu.VMEM((rows, c1), BF16),
+            pltpu.VMEM((n, half, c2), BF16),
+            pltpu.VMEM((c2 // 128, rows, 128), jnp.float32),
             dma(3), dma(3), dma(3), dma(3), dma(n), dma(n), dma(n), dma(n),
-            dma(n - 1), dma(n - 1), dma(2),
+            dma(n), dma(n), dma(n), dma(2),
             *turn_scratch(n),
         ],
-        dec_part, stem_pad[2 : 2 + rows], targets, pool_pad,
+        dec_part, stem_pad[2 : 2 + rows], targets, pool,
     )
     slope_pad = jnp.concatenate(
         [slope_chan[j, EDGE - 2 : EDGE + rows + 2] for j in range(n)], axis=1
     )
-    up_grad = jnp.zeros((rows, c2), jnp.float32)
-    for k in range(KW):
-        up_grad = up_grad + jnp.dot(
-            slope_pad[4 - k : 4 - k + rows], w_dec[:, k, :], preferred_element_type=jnp.float32
-        )
-    pool_grad = up_grad.reshape(half, 2, -1).sum(axis=1)
-    act_grad = 0.5 * jnp.repeat(pool_grad, 2, axis=0)
-    pre_grad = (act_grad * gelu_slope(enc_pre)).astype(BF16)
+    up_grad = lax.dot_general(
+        windows(slope_pad)[::-1], w_dec, (((0, 2), (1, 0)), ((), ())),
+        preferred_element_type=jnp.float32,
+    )
     pre_seq = call(
         functools.partial(turn_kernel, n), 3, struct((n, rows, c2), BF16),
-        turn_scratch(n), pre_grad,
-    )
-    up_all = jnp.pad(jnp.repeat(pool_all.reshape(length // 2, c2), 2, axis=0), ((2, 2), (0, 0)))
+        [pltpu.VMEM((rows, c2), BF16), *turn_scratch(n)], up_grad, enc_pre,
+    )
+    up_all = jnp.pad(up_all.reshape(length, c2), ((2, 2), (0, 0)))
     g_dec = all_rows_grad(slope_seq.reshape(length, c1), up_all)
     g_enc = all_rows_grad(pre_seq.reshape(length, c2), stem_all)
     return (pred, g_enc, g_dec)

time: 159 us -> 142 us (0.89)
  matrix products: 43.5 us -> 17.5 us
  local copies, waits for them, and re-layouts: 17.8 us -> 31.3 us
  Pallas kernels: 94.5 us -> 91.3 us
    dot_general x15 -> x3, matrix products: 36.5 us -> 9.79 us  [the longest x1 5.27 us: square_shards(): lax.dot_general(windows(slope_pad)[::-1], w_dec, (((0, 2), (1, 0)), ((),...]
    unnamed x28 -> x50, local copies, waits for them, and re-layouts: 5.67 us -> 19.5 us
    reshape x3 -> x0, local copies, waits for them, and re-layouts: 4.71 us -> none  [the longest x1 3.67 us: square_shards(): jnp.repeat(pool_all.reshape(length // 2, c2), 2, axis=0)]
    rev x0 -> x1, local copies, waits for them, and re-layouts: none -> 4.25 us  [square_shards(): windows(slope_pad)[::-1]]
    pallas_call x4, Pallas kernels: 94.5 us -> 91.3 us  [call(): pl.pallas_call(kernel, out_shape=outs, in_specs=[vmem] * len(operands), o...]
    broadcast_in_dim x6 -> x0, local copies, waits for them, and re-layouts: 3.07 us -> none  [the longest x1 1.97 us: square_shards(): jnp.repeat(pool_all.reshape(length // 2, c2), 2, axis=0)]
    reshape x1, local copies, waits for them, and re-layouts: 0.51 us -> 2.21 us  [square_shards(): dec_part = dec_part.reshape(rows, n, c1).transpose(1, 0, 2)]
where the time goes in v3:
time: 142 us; the launch traced here: 141 us
  Pallas kernels  91.3 us (64%)
  local copies, waits for them, and re-layouts  31.3 us (22%)
  matrix products  17.5 us (12%)
    pallas_call x4, Pallas kernels, call(): pl.pallas_call(kernel, out_shape=outs, in_specs=[vmem] * len(operands), o...  91.3 us
    unnamed x50, local copies, waits for them, and re-layouts  19.5 us
    dot_general x10, matrix products, all_rows_grad(): lax.dot_general(cotangent, padded[k:k + count], (((0,), (0,)), ((), ())),...  6.12 us
    dot_general x1, matrix products, square_shards(): lax.dot_general(windows(slope_pad)[::-1], w_dec, (((0, 2), (1, 0)), ((),...  5.27 us
    dot_general x2, matrix products, conv_stack(): lax.dot_general(windows(padded), weight, (((0, 2), (1, 2)), ((), ())), pr...  4.52 us
    rev x1, local copies, waits for them, and re-layouts, square_shards(): windows(slope_pad)[::-1]  4.25 us

profile of v3, /device:TPU:0, one launch (start us, length us, event | category | flops | bytes accessed | tf_op | source)
XLA Modules:
  0.0 141.4 jit_solution(7235366080879798155)
XLA Ops:
  0.7 0.8 copy-done.12
  1.5 7.3 %shard_map.76 = s32[4,4,128]{2,1,0:T(4,128)S(1)} custom-call(s32[4,128]{1,0:T(4,128)S(1)} %bitcast.160), custom_call_target="tpu_custom_call" | custom-call | tf_op jit(solution)/shard_map/pallas_call | solution.py:486
  8.9 1.1 copy.40.target_ref
  10.0 1.6 %fusion.5 = bf16[2048,192]{1,0:T(8,128)(2,1)S(1)} fusion(s32[5,2048]{1,0:T(8,128)S(1)} %stack.113, bf16[192,5,4]{0,2,1:T(4,128)(2,1)} %param.6), kind=kOutput, calls=%fused_computation.8 | convolution fusion | flops 19308544 | bytes 835072 | tf_op jit(solution)/shard_map/dot_general | solution.py:539
  12.7 1.8 %fusion.part_ref = bf16[512,1536]{1,0:T(8,128)(2,1)S(1)} fusion(bf16[5,512,192]{2,1,0:T(8,128)(2,1)S(1)} %fusion.57, bf16[1536,5,192]{0,2,1:T(8,128)(2,1)S(1)} %copy-done), kind=kOutput, calls=%fused_computation.2 | convolution fusion | flops 1510735872 | bytes 5505024 | tf_op jit(solution)/shard_map/dot_general | solution.py:508
  14.5 19.0 %shard_map.77 = (f32[512,384]{1,0:T(8,128)S(1)}, bf16[544,384]{1,0:T(8,128)(2,1)S(1)}, bf16[256,384]{1,0:T(8,128)(2,1)S(1)}) custom-call(bf16[512,1536]{1,0:T(8,128)(2,1)S(1)} %fusion.part_ref), custom_call_target="tpu_custom_call" | custom-call | tf_op jit(solution)/shard_map/pallas_call | solution.py:486
  33.5 0.9 copy-done.7
  34.5 0.7 copy-done.10
  35.8 1.3 copy-done.15
  37.1 2.7 %bitcast_convert_fusion = bf16[512,768]{1,0:T(8,128)(2,1)} fusion(bf16[5,512,384]{2,1,0:T(8,128)(2,1)S(1)} %bitcast_dynamic-update-slice_fusion, bf16[768,5,384]{2,0,1:T(8,128)(2,1)S(1)} %copy-done.15), kind=kOutput, calls=%fused_computation.9 | convolution fusion | flops 1510342656 | bytes 5701632 | tf_op jit(solution)/shard_map/dot_general | solution.py:508
  39.8 2.3 %copy.38 = bf16[512,768]{0,1:T(8,128)(2,1)} copy(bf16[512,768]{1,0:T(8,128)(2,1)} %bitcast_convert_fusion) | data formatting | bytes 1572864 | tf_op jit(solution)/shard_map/convert_element_type | solution.py:563
  42.1 2.2 %copy.39 = bf16[512,4,192]{2,0,1:T(8,128)(2,1)} copy(bf16[512,4,192]{0,2,1:T(8,128)(2,1)} %bitcast.161) | data formatting | bytes 1572864 | tf_op jit(solution)/shard_map/reshape | solution.py:564
  44.3 1.2 copy-done.5
  45.5 0.9 copy-done.11
  46.5 37.4 %shard_map.78 = (bf16[512,192]{1,0:T(8,128)(2,1)S(1)}, bf16[4,544,192]{2,1,0:T(8,128)(2,1)S(1)}, bf16[4,512,192]{2,1,0:T(8,128)(2,1)S(1)}, bf16[4,512,384]{2,1,0:T(8,128)(2,1)S(1)}) custom-call(bf16[4,512,192]{2,1,0:T(8,128)(2,1)S(1)} %bitcast.152, bf16[512,192]{1,0:T(8,128)(2,1)S(1)} %get-tuple-element.27.stem_ref, bf16[512,192]{1,0:T(8,128)(2,1)S(1)} %copy.40.target_ref, ...), custom_call_target="tpu_custom_call" | custom-call | tf_op jit(solution)/shard_map/pallas_call | solution.py:486
  83.9 1.2 copy-done.1
  85.0 1.0 copy-done.3
  86.0 1.0 copy-done.6
  87.0 0.7 copy-done.9
  87.7 1.8 %copy.42 = bf16[512,192]{0,1:T(8,128)(2,1)} copy(bf16[512,192]{1,0:T(8,128)(2,1)} %copy-done.9) | data formatting | bytes 393216
  89.5 1.6 %slice_bitcast_fusion.8 = (bf16[516,192]{1,0:T(8,128)(2,1)S(1)}, bf16[516,192]{1,0:T(8,128)(2,1)S(1)}, bf16[516,192]{1,0:T(8,128)(2,1)S(1)}, bf16[516,192]{1,0:T(8,128)(2,1)S(1)}) fusion(bf16[4,544,192]{2,1,0:T(8,128)(2,1)} %copy-done.6), kind=kLoop, calls=%fused_computation.66 | loop fusion | bytes 1585152 | tf_op jit(solution)/shard_map/squeeze | solution.py:586
  94.6 1.0 fusion.56
  95.6 1.1 fusion.55
  96.7 1.1 fusion.54
  97.8 1.1 fusion.53
  98.9 1.1 fusion.52
  99.9 4.2 %rev.3 = bf16[5,512,768]{2,1,0:T(8,128)(2,1)} reverse(bf16[5,512,768]{2,1,0:T(8,128)(2,1)} %fusion.52), dimensions={0} | reverse | bytes 7864320 | tf_op jit(solution)/shard_map/rev | solution.py:589
  104.2 5.3 %convolution_bitcast_fusion.2.grad_ref = f32[512,384]{1,0:T(8,128)S(1)} fusion(bf16[5,512,768]{2,1,0:T(8,128)(2,1)} %rev.3, bf16[768,5,384]{2,0,1:T(8,128)(2,1)} %param.8), kind=kOutput, calls=%fused_computation.18 | convolution fusion | flops 1509949440 | bytes 7667712 | tf_op jit(solution)/shard_map/dot_general | solution.py:588
  109.5 27.6 %shard_map.79 = bf16[4,512,384]{2,1,0:T(8,128)(2,1)S(1)} custom-call(f32[512,384]{1,0:T(8,128)S(1)} %convolution_bitcast_fusion.2.grad_ref, f32[512,384]{1,0:T(8,128)S(1)} %copy-done.8), custom_call_target="tpu_custom_call" | custom-call | tf_op jit(solution)/shard_map/pallas_call | solution.py:486
  137.1 0.6 fusion.31
  139.0 0.6 fusion.28
  140.3 1.1 copy-done.17
  (46 shorter events, 7.1 us)
Async XLA Ops:
  0.6 12.0 %copy-start = (bf16[1536,5,192]{0,2,1:T(8,128)(2,1)S(1)}, bf16[1536,5,192]{0,2,1:T(8,128)(2,1)}, u32[]{:S(2)}) copy-start(bf16[1536,5,192]{0,2,1:T(8,128)(2,1)} %param.7) | copy-start | bytes 8847364
  0.7 0.8 copy-start.12
  11.6 1.0 copy-start.13
  33.5 0.9 copy-start.7
  34.5 0.7 copy-start.10
  35.3 1.8 %copy-start.15 = (bf16[768,5,384]{2,0,1:T(8,128)(2,1)S(1)}, bf16[768,5,384]{2,0,1:T(8,128)(2,1)}, u32[]{:S(2)}) copy-start(bf16[768,5,384]{2,0,1:T(8,128)(2,1)} %param.8) | copy-start | bytes 8847364
  44.3 1.2 copy-start.5
  45.5 0.9 copy-start.11
  83.9 1.2 copy-start.1
  85.0 1.0 copy-start.3
  86.0 1.0 copy-start.6
  87.0 0.7 copy-start.9
  89.5 1.9 %copy-start.2 = (bf16[4,512,384]{2,1,0:T(8,128)(2,1)S(1)}, bf16[4,512,384]{2,1,0:T(8,128)(2,1)}, u32[]{:S(2)}) copy-start(bf16[4,512,384]{2,1,0:T(8,128)(2,1)} %copy-done.1) | copy-start | bytes 4718596
  89.5 2.0 %copy-start.4 = (bf16[4,512,192]{2,1,0:T(8,128)(2,1)S(1)}, bf16[4,512,192]{2,1,0:T(8,128)(2,1)}, u32[]{:S(2)}) copy-start(bf16[4,512,192]{2,1,0:T(8,128)(2,1)} %copy-done.3) | copy-start | bytes 2359300
  94.6 2.1 %copy-start.16 = (f32[192,5,384]{2,0,1:T(8,128)}, f32[192,5,384]{2,0,1:T(8,128)S(1)}, u32[]{:S(2)}) copy-start(f32[192,5,384]{2,0,1:T(8,128)S(1)} %fusion.41) | copy-start | bytes 4423684
  104.2 5.3 %copy-start.8 = (f32[512,384]{1,0:T(8,128)S(1)}, f32[512,384]{1,0:T(8,128)}, u32[]{:S(2)}) copy-start(f32[512,384]{1,0:T(8,128)} %copy-done.7) | copy-start | bytes 2359300
  109.5 27.6 %copy-start.14 = (bf16[2048,192]{1,0:T(8,128)(2,1)S(1)}, bf16[2048,192]{1,0:T(8,128)(2,1)}, u32[]{:S(2)}) copy-start(bf16[2048,192]{1,0:T(8,128)(2,1)} %copy-done.13) | copy-start | bytes 2359300
  140.3 1.1 copy-start.17

commit v4 on v3

--- a/solution.py
+++ b/solution.py
@@ -125,6 +125,8 @@
 MESH_ID = pl.DeviceIdType.MESH
 BF16 = jnp.bfloat16
 EDGE = 16
+CHUNKS = 4
+STEP = 64
 VMEM_BYTES = 8 * 1024 * 1024
 
 
@@ -218,10 +220,12 @@
         return send(self.out.at[slot, at], self.out.at[slot, at], self.share_send.at[index],
                     self.share_recv.at[index], self.s, to)
 
-    def finish(self, between=None):
-        mate, across, far = partners(self.c)
-        slots = [lax.rem(self.s + d, self.n) for d in range(self.n)]
-        for d, slot in enumerate(slots):
+    def slots(self):
+        return [lax.rem(self.s + d, self.n) for d in range(self.n)]
+
+    def forward(self):
+        mate, across, _ = partners(self.c)
+        for d, slot in enumerate(self.slots()):
             if d == 0:
                 pl.when(self.s == self.c)(lambda: self.keep().wait())
                 pl.when(self.s != self.c)(lambda: self.quarter(self.c, slot).wait_recv())
@@ -229,49 +233,64 @@
                 self.quarter(self.c, slot).wait_recv()
             self.share(slot, 1, self.c, across).start()
             self.share(slot, 0, self.c, mate).start()
-        if between is not None:
-            between()
-        for slot in slots:
+
+    def relay(self):
+        mate, across, _ = partners(self.c)
+        for slot in self.slots():
             self.share(slot, 1, across, across).wait_recv()
             self.share(slot, 2, across, mate).start()
-        for slot in slots:
+
+    def finish(self):
+        mate, across, far = partners(self.c)
+        for slot in self.slots():
             self.share(slot, 0, mate, mate).wait_recv()
             self.share(slot, 2, far, mate).wait_recv()
-        for slot in slots:
             self.share(slot, 0, self.c, mate).wait_send()
             self.share(slot, 1, self.c, across).wait_send()
             self.share(slot, 2, across, mate).wait_send()
         self.each(lambda q: self.quarter(q, self.s).wait_send(), None)
 
 
-def pair_sum(block, held, pair, s, c, rows, send_sem, recv_sem, finish):
+def pair_sum(block, held, pair, s, c, rows, send_sem, recv_sem, finish, done):
     mate, across, far = partners(c)
-    first = send(block(far), held.at[1], send_sem.at[1], recv_sem.at[1], s, mate)
-    second = send(block(mate), held.at[0], send_sem.at[0], recv_sem.at[0], s, mate)
-    last = send(pair, held.at[2], send_sem.at[2], recv_sem.at[2], s, across)
-    first.start()
-    second.start()
-    step = 64
-    first.wait_recv()
-
-    @pl.loop(0, rows // step)
-    def _(i):
-        at = pl.ds(pl.multiple_of(i * step, step), step)
+    piece = rows // CHUNKS
+    sources = (block(mate), block(far), pair)
+    targets = (mate, mate, across)
+
+    def hop(kind, q):
+        at = pl.ds(q * piece, piece)
+        index = kind * CHUNKS + q
+        return send(sources[kind].at[at], held.at[kind, at], send_sem.at[index],
+                    recv_sem.at[index], s, targets[kind])
+
+    def steps(q, body):
+        @pl.loop(0, piece // STEP)
+        def _(i):
+            body(pl.ds(pl.multiple_of(q * piece + i * STEP, STEP), STEP))
+
+    def pair_rows(at):
         pair[at, :] = (
             block(across)[at, :].astype(jnp.float32) + held[1, at, :].astype(jnp.float32)
         ).astype(BF16)
 
-    last.start()
-    second.wait_recv()
-    last.wait_recv()
-
-    @pl.loop(0, rows // step)
-    def _(i):
-        at = pl.ds(pl.multiple_of(i * step, step), step)
+    def total_rows(at):
         total = block(c)[at, :].astype(jnp.float32) + held[0, at, :].astype(jnp.float32)
         finish(at, total + held[2, at, :].astype(jnp.float32))
 
-    return [first, second, last]
+    for q in range(CHUNKS):
+        hop(1, q).start()
+    for q in range(CHUNKS):
+        hop(0, q).start()
+    for q in range(CHUNKS):
+        hop(1, q).wait_recv()
+        steps(q, pair_rows)
+        hop(2, q).start()
+    for q in range(CHUNKS):
+        hop(0, q).wait_recv()
+        hop(2, q).wait_recv()
+        steps(q, total_rows)
+        done(q)
+    return [hop(kind, q) for kind in range(3) for q in range(CHUNKS)]
 
 
 def pair_add(value):
@@ -306,7 +325,9 @@
         for j in range(width // 128):
             wide[j, at, :] = pooled[:, j * 128 : (j + 1) * 128].astype(jnp.float32)
 
-    copies = pair_sum(block, held, pair, s, c, rows, send_sem, recv_sem, finish)
+    copies = pair_sum(
+        block, held, pair, s, c, rows, send_sem, recv_sem, finish, lambda q: None
+    )
     up = send(up_ref.at[pl.ds(rows, EDGE)], up_ref.at[pl.ds(0, EDGE)], edge_send.at[0],
               edge_recv.at[0], lax.rem(s + 1, n), c)
     down = send(up_ref.at[pl.ds(EDGE, EDGE)], up_ref.at[pl.ds(rows + EDGE, EDGE)],
@@ -371,81 +392,65 @@
 
 
 def slope_kernel(
-    n, scale, part_ref, stem_ref, target_ref, pool_ref, pred_ref, chan_ref, seq_ref, up_ref,
-    held, pair, slope, all_ref, wide, send_sem, recv_sem, row_send, row_recv, lo_send, lo_recv, hi_send, hi_recv,
-    right_send, left_send, pool_recv, local_sem, *turn_sems,
+    n, scale, part_ref, stem_ref, target_ref, pool_ref, pred_ref, chan_ref, all_ref,
+    held, pair, send_sem, recv_sem, row_send, row_recv, lo_send, lo_recv, hi_send, hi_recv,
+    right_send, left_send, pool_recv, local_sem,
 ):
     s, c = lax.axis_index("seq"), lax.axis_index("chan")
     rows, width = pred_ref.shape
+    piece = rows // CHUNKS
     mate, across, far = partners(c)
     greet(whole_group(n, s, c))
-    half, up_width = pool_ref.shape
-    pools = PoolRelay(
-        n, s, c, pool_ref, all_ref, right_send, left_send, pool_recv, local_sem.at[1]
-    )
+    pools = PoolRelay(n, s, c, pool_ref, all_ref, right_send, left_send, pool_recv, local_sem)
+    up, down = lax.rem(s + 1, n), lax.rem(s + n - 1, n)
 
     def finish(at, total):
         output = total + stem_ref[at, :].astype(jnp.float32)
         pred_ref[at, :] = output.astype(BF16)
-        slope[at, :] = ((output - target_ref[at, :].astype(jnp.float32)) * scale).astype(BF16)
-
-    pools.start()
-    copies = pair_sum(
-        lambda j: part_ref.at[j], held, pair, s, c, rows, send_sem, recv_sem, finish
-    )
-    pools.arrive(1)
-    core = pl.ds(EDGE, rows)
-    up, down = lax.rem(s + 1, n), lax.rem(s + n - 1, n)
-
-    def row_copy(index, src, owner, to):
-        return send(src, chan_ref.at[owner, core], row_send.at[index], row_recv.at[index], s, to)
-
-    to_across = row_copy(1, slope, c, across)
-    to_mate = row_copy(0, slope, c, mate)
-    relay = row_copy(2, chan_ref.at[across, core], across, mate)
+        spot = pl.ds(pl.multiple_of(at.start + EDGE, EDGE), at.size)
+        chan_ref[c, spot, :] = ((output - target_ref[at, :].astype(jnp.float32)) * scale).astype(BF16)
+
+    def row_copy(kind, q, owner, to):
+        spot = chan_ref.at[owner, pl.ds(EDGE + q * piece, piece)]
+        index = kind * CHUNKS + q
+        return send(spot, spot, row_send.at[index], row_recv.at[index], s, to)
+
     lo_copies, hi_copies = [], []
     for d in range(n):
         p = lax.rem(c + d, n)
         lo_copies.append(
-            send(slope.at[pl.ds(rows - EDGE, EDGE)], chan_ref.at[c, pl.ds(0, EDGE)],
+            send(chan_ref.at[c, pl.ds(rows, EDGE)], chan_ref.at[c, pl.ds(0, EDGE)],
                  lo_send.at[d], lo_recv.at[d], up, p)
         )
         hi_copies.append(
-            send(slope.at[pl.ds(0, EDGE)], chan_ref.at[c, pl.ds(EDGE + rows, EDGE)],
+            send(chan_ref.at[c, pl.ds(EDGE, EDGE)], chan_ref.at[c, pl.ds(EDGE + rows, EDGE)],
                  hi_send.at[d], hi_recv.at[d], down, p)
         )
-    for copy in [to_across, to_mate] + lo_copies + hi_copies:
-        copy.start()
-    mine = pltpu.make_async_copy(slope, chan_ref.at[c, core], local_sem.at[0])
-    mine.start()
-    turn = Turn(n, s, c, slope, seq_ref, turn_sems)
-    turn.start()
+
+    def done(q):
+        row_copy(1, q, c, across).start()
+        row_copy(0, q, c, mate).start()
+        if q == 0:
+            for copy in hi_copies:
+                copy.start()
+        if q == CHUNKS - 1:
+            for copy in lo_copies:
+                copy.start()
+
+    pools.start()
+    copies = pair_sum(
+        lambda j: part_ref.at[j], held, pair, s, c, rows, send_sem, recv_sem, finish, done
+    )
+    pools.arrive(1)
+    for q in range(CHUNKS):
+        row_copy(1, q, across, across).wait_recv()
+        row_copy(2, q, across, mate).start()
     pools.arrive(2)
-    to_across.wait_recv()
-    relay.start()
-
-    def upsample():
-        pools.arrive(3)
-        pools.end()
-
-        @pl.loop(0, n)
-        def _(slot):
-            for j in range(up_width // 128):
-                lanes = slice(j * 128, (j + 1) * 128)
-                value = all_ref[slot, :, lanes].astype(jnp.float32)
-                wide[j, pl.ds(0, half, stride=2), :] = value
-                wide[j, pl.ds(1, half, stride=2), :] = value
-                up_ref[slot, :, lanes] = wide[j].astype(BF16)
-
-    turn.finish(upsample)
-    to_across.wait_send()
-    to_mate.wait()
-    relay.wait()
+    for q in range(CHUNKS):
+        row_copy(0, q, mate, mate).wait_recv()
+        row_copy(2, q, far, mate).wait_recv()
     for copy in lo_copies + hi_copies:
         copy.wait()
-    mine.wait()
-    for copy in copies:
-        copy.wait_send()
     blank = jnp.zeros((EDGE, width), BF16)
 
     @pl.when(s == 0)
@@ -458,22 +463,51 @@
         for j in range(n):
             chan_ref[j, EDGE + rows :, :] = blank
 
-
-def turn_kernel(n, grad_ref, pre_ref, seq_ref, own, *turn_sems):
+    pools.arrive(3)
+    pools.end()
+    for q in range(CHUNKS):
+        row_copy(0, q, c, mate).wait_send()
+        row_copy(1, q, c, across).wait_send()
+        row_copy(2, q, across, mate).wait_send()
+    for copy in copies:
+        copy.wait_send()
+
+
+def turn_kernel(
+    n, grad_ref, pre_ref, chan_ref, all_ref, pre_seq_ref, slope_seq_ref, up_ref, own, wide, *sems
+):
     s, c = lax.axis_index("seq"), lax.axis_index("chan")
+    rows = own.shape[0]
+    half, up_width = all_ref.shape[1:]
     greet(whole_group(n, s, c))
-    turn = Turn(n, s, c, own, seq_ref, turn_sems)
-    step = 64
-    pieces = turn.piece // step
-
-    def slope_rows(first):
-        @pl.loop(0, pieces)
+    slope_own = chan_ref.at[c, pl.ds(EDGE, rows)]
+    slope_turn = Turn(n, s, c, slope_own, slope_seq_ref, sems[: len(sems) // 2])
+    turn = Turn(n, s, c, own, pre_seq_ref, sems[len(sems) // 2 :])
+
+    def pre_rows(first):
+        @pl.loop(0, turn.piece // STEP)
         def _(i):
-            at = pl.ds(pl.multiple_of(first + i * step, step), step)
+            at = pl.ds(pl.multiple_of(first + i * STEP, STEP), STEP)
             grad = 0.5 * pair_add(grad_ref[at, :])
             own[at, :] = (grad * gelu_slope(pre_ref[at, :])).astype(BF16)
 
-    turn.start(slope_rows)
+    slope_turn.start()
+    turn.start(pre_rows)
+    slope_turn.forward()
+    turn.forward()
+
+    @pl.loop(0, n)
+    def _(slot):
+        for j in range(up_width // 128):
+            lanes = slice(j * 128, (j + 1) * 128)
+            value = all_ref[slot, :, lanes].astype(jnp.float32)
+            wide[j, pl.ds(0, half, stride=2), :] = value
+            wide[j, pl.ds(1, half, stride=2), :] = value
+            up_ref[slot, :, lanes] = wide[j].astype(BF16)
+
+    slope_turn.relay()
+    turn.relay()
+    slope_turn.finish()
     turn.finish()
 
 
@@ -555,43 +589,51 @@
             pltpu.VMEM((n - 1, rows, c2), BF16),
             pltpu.VMEM((rows, c2), BF16),
             pltpu.VMEM((c2 // 128, rows, 128), jnp.float32),
-            dma(3), dma(3), dma(2), dma(2),
+            dma(3 * CHUNKS), dma(3 * CHUNKS), dma(2), dma(2),
         ],
         part,
     )
     up_pad = up_own[EDGE - 2 : EDGE + rows + 2]
-    dec_part = conv_stack(up_pad, w_dec).astype(BF16)
-    dec_part = dec_part.reshape(rows, n, c1).transpose(1, 0, 2)
-    pred, slope_chan, slope_seq, up_all = call(
+    dec_part = jnp.stack(
+        [conv_stack(up_pad, w_dec[j * c1 : (j + 1) * c1]).astype(BF16) for j in range(n)]
+    )
+    pred, slope_chan, pool_all = call(
         functools.partial(slope_kernel, n, 1.0 / math.sqrt(length)), 2,
         (
             struct((rows, c1), BF16),
             struct((n, rows + 2 * EDGE, c1), BF16),
+            struct((n, half, c2), BF16),
+        ),
+        [
+            pltpu.VMEM((n - 1, rows, c1), BF16),
+            pltpu.VMEM((rows, c1), BF16),
+            dma(3 * CHUNKS), dma(3 * CHUNKS), dma(3 * CHUNKS), dma(3 * CHUNKS),
+            dma(n), dma(n), dma(n), dma(n), dma(n), dma(n), dma(n),
+            pltpu.SemaphoreType.DMA,
+        ],
+        dec_part, stem_pad[2 : 2 + rows], targets, pool,
+    )
+    slope_pad = jnp.concatenate(
+        [slope_chan[j, EDGE - 2 : EDGE + rows + 2] for j in range(n)], axis=1
+    )
+    up_grad = jnp.zeros((rows, c2), jnp.float32)
+    for k in range(KW):
+        up_grad = up_grad + jnp.dot(
+            slope_pad[4 - k : 4 - k + rows], w_dec[:, k, :], preferred_element_type=jnp.float32
+        )
+    pre_seq, slope_seq, up_all = call(
+        functools.partial(turn_kernel, n), 3,
+        (
+            struct((n, rows, c2), BF16),
             struct((n, rows, c1), BF16),
             struct((n, rows, c2), BF16),
         ),
         [
-            pltpu.VMEM((n - 1, rows, c1), BF16),
-            pltpu.VMEM((rows, c1), BF16),
-            pltpu.VMEM((rows, c1), BF16),
-            pltpu.VMEM((n, half, c2), BF16),
+            pltpu.VMEM((rows, c2), BF16),
             pltpu.VMEM((c2 // 128, rows, 128), jnp.float32),
-            dma(3), dma(3), dma(3), dma(3), dma(n), dma(n), dma(n), dma(n),
-            dma(n), dma(n), dma(n), dma(2),
-            *turn_scratch(n),
+            *turn_scratch(n), *turn_scratch(n),
         ],
-        dec_part, stem_pad[2 : 2 + rows], targets, pool,
-    )
-    slope_pad = jnp.concatenate(
-        [slope_chan[j, EDGE - 2 : EDGE + rows + 2] for j in range(n)], axis=1
-    )
-    up_grad = lax.dot_general(
-        windows(slope_pad)[::-1], w_dec, (((0, 2), (1, 0)), ((), ())),
-        preferred_element_type=jnp.float32,
-    )
-    pre_seq = call(
-        functools.partial(turn_kernel, n), 3, struct((n, rows, c2), BF16),
-        [pltpu.VMEM((rows, c2), BF16), *turn_scratch(n)], up_grad, enc_pre,
+        up_grad, enc_pre, slope_chan, pool_all,
     )
     up_all = jnp.pad(up_all.reshape(length, c2), ((2, 2), (0, 0)))
     g_dec = all_rows_grad(slope_seq.reshape(length, c1), up_all)
@@ -604,7 +646,7 @@
     rows, c1, c2 = dna_bases.shape[0], w_stem.shape[0], w_dec.shape[2]
     n = lax.axis_size("seq")
     square = n == 4 and lax.axis_size("chan") == 4
-    if square and rows % 128 == 0 and c2 % 128 == 0 and c1 % 64 == 0:
+    if square and rows % (CHUNKS * STEP) == 0 and c2 % 128 == 0 and c1 % 64 == 0:
         return square_shards(*args)
     return general_shards(*args)
 

time: 142 us -> 120 us (0.85)
  local copies, waits for them, and re-layouts: 31.3 us -> 13.7 us
  Pallas kernels: 91.3 us -> 89.1 us
  matrix products: 17.5 us -> 15.4 us
    unnamed x50 -> x38, local copies, waits for them, and re-layouts: 19.5 us -> 11.7 us
    rev x1 -> x0, local copies, waits for them, and re-layouts: 4.25 us -> none  [square_shards(): windows(slope_pad)[::-1]]
    dot_general x1 -> x5, matrix products: 5.27 us -> 2.9 us  [square_shards(): jnp.dot(slope_pad[4 - k:4 - k + rows], w_dec[:, k, :], preferred_element_...]
    convert_element_type x1 -> x0, local copies, waits for them, and re-layouts: 2.3 us -> none  [square_shards(): dec_part = conv_stack(up_pad, w_dec).astype(BF16)]
    reshape x1 -> x0, local copies, waits for them, and re-layouts: 2.21 us -> none  [square_shards(): dec_part = dec_part.reshape(rows, n, c1).transpose(1, 0, 2)]
    pallas_call x4, Pallas kernels: 91.3 us -> 89.1 us  [call(): pl.pallas_call(kernel, out_shape=outs, in_specs=[vmem] * len(operands), o...]
    dot_general x2 -> x5, matrix products: 4.52 us -> 4.73 us  [conv_stack(): lax.dot_general(windows(padded), weight, (((0, 2), (1, 2)), ((), ())), pr...]
where the time goes in v4:
time: 120 us
  Pallas kernels  89.1 us (74%)
  matrix products  15.4 us (13%)
  local copies, waits for them, and re-layouts  13.7 us (11%)
    pallas_call x4, Pallas kernels, call(): pl.pallas_call(kernel, out_shape=outs, in_specs=[vmem] * len(operands), o...  89.1 us
    unnamed x38, local copies, waits for them, and re-layouts  11.7 us
    dot_general x10, matrix products, all_rows_grad(): lax.dot_general(cotangent, padded[k:k + count], (((0,), (0,)), ((), ())),...  6.11 us
    dot_general x5, matrix products, conv_stack(): lax.dot_general(windows(padded), weight, (((0, 2), (1, 2)), ((), ())), pr...  4.73 us
    dot_general x5, matrix products, square_shards(): jnp.dot(slope_pad[4 - k:4 - k + rows], w_dec[:, k, :], preferred_element_...  2.9 us

profile of v4, /device:TPU:0, one launch (start us, length us, event | category | flops | bytes accessed | tf_op | source)
XLA Modules:
  0.0 119.7 jit_solution(11991231912394095511)
XLA Ops:
  0.7 0.8 copy-done.7
  1.5 7.3 %shard_map.76 = s32[4,4,128]{2,1,0:T(4,128)S(1)} custom-call(s32[4,128]{1,0:T(4,128)S(1)} %bitcast.175), custom_call_target="tpu_custom_call" | custom-call | tf_op jit(solution)/shard_map/pallas_call | solution.py:520
  8.9 1.1 copy.34.target_ref
  10.0 1.6 %fusion.5 = bf16[2048,192]{1,0:T(8,128)(2,1)S(1)} fusion(s32[5,2048]{1,0:T(8,128)S(1)} %stack.128, bf16[192,5,4]{0,2,1:T(4,128)(2,1)} %param.6), kind=kOutput, calls=%fused_computation.8 | convolution fusion | flops 19308544 | bytes 835072 | tf_op jit(solution)/shard_map/dot_general | solution.py:573
  12.0 0.6 copy-done.8
  12.7 1.8 %fusion.part_ref = bf16[512,1536]{1,0:T(8,128)(2,1)S(1)} fusion(bf16[5,512,192]{2,1,0:T(8,128)(2,1)S(1)} %fusion.80, bf16[1536,5,192]{0,2,1:T(8,128)(2,1)S(1)} %copy-done), kind=kOutput, calls=%fused_computation.2 | convolution fusion | flops 1510735872 | bytes 5505024 | tf_op jit(solution)/shard_map/dot_general | solution.py:542
  14.5 18.1 %shard_map.77 = (f32[512,384]{1,0:T(8,128)S(1)}, bf16[544,384]{1,0:T(8,128)(2,1)S(1)}, bf16[256,384]{1,0:T(8,128)(2,1)S(1)}) custom-call(bf16[512,1536]{1,0:T(8,128)(2,1)S(1)} %fusion.part_ref), custom_call_target="tpu_custom_call" | custom-call | tf_op jit(solution)/shard_map/pallas_call | solution.py:520
  32.6 0.9 copy-done.3
  34.1 1.3 %copy-done.10 = bf16[768,5,384]{2,0,1:T(8,128)(2,1)S(1)} copy-done((bf16[768,5,384]{2,0,1:T(8,128)(2,1)S(1)}, bf16[768,5,384]{2,0,1:T(8,128)(2,1)}, u32[]{:S(2)}) %copy-start.10) | copy-done | bytes 2949144
  35.5 0.7 fusion.48
  36.2 0.7 fusion.49
  36.9 0.7 fusion.50
  37.7 0.7 fusion.51
  38.6 24.3 %shard_map.78 = (bf16[512,192]{1,0:T(8,128)(2,1)S(1)}, bf16[4,544,192]{2,1,0:T(8,128)(2,1)S(1)}, bf16[4,256,384]{2,1,0:T(8,128)(2,1)S(1)}) custom-call(bf16[4,512,192]{2,1,0:T(8,128)(2,1)S(1)} %pad_maximum_fusion.part_ref, bf16[512,192]{1,0:T(8,128)(2,1)S(1)} %get-tuple-element.28.stem_ref, bf16[512,192]{1,0:T(8,128)(2,1)S(1)} %copy.34.target_ref, ...), custom_call_target="tpu_custom_call" | custom-call | tf_op jit(solution)/shard_map/pallas_call | solution.py:520
  62.9 1.0 copy-done.1
  63.9 0.9 copy-done.5
  64.8 0.8 copy.36
  65.6 1.6 %slice_bitcast_fusion.3 = (bf16[516,192]{1,0:T(8,128)(2,1)S(1)}, bf16[516,192]{1,0:T(8,128)(2,1)S(1)}, bf16[516,192]{1,0:T(8,128)(2,1)S(1)}, bf16[516,192]{1,0:T(8,128)(2,1)S(1)}) fusion(bf16[4,544,192]{2,1,0:T(8,128)(2,1)} %copy-done.1), kind=kLoop, calls=%fused_computation.91 | loop fusion | bytes 1585152 | tf_op jit(solution)/shard_map/squeeze | solution.py:617
  70.7 0.6 copy-done.2
  71.8 39.5 %shard_map.79 = (bf16[4,512,384]{2,1,0:T(8,128)(2,1)S(1)}, bf16[4,512,192]{2,1,0:T(8,128)(2,1)S(1)}, bf16[4,512,384]{2,1,0:T(8,128)(2,1)S(1)}) custom-call(f32[512,384]{1,0:T(8,128)S(1)} %convolution_add_fusion.grad_ref, f32[512,384]{1,0:T(8,128)S(1)} %copy-done.4, bf16[4,544,192]{2,1,0:T(8,128)(2,1)S(1)} %copy-done.2, bf16[4,256,384]{2,1,0:T(8,128)(2,1)S(1)} %copy-done.6), custom_call_target="tpu_custom_call" | custom-call | tf_op jit(solution)/shard_map/pallas_call | solution.py:520
  111.3 0.6 fusion.21
  111.9 0.6 fusion.27
  112.6 0.6 fusion.30
  113.2 0.6 fusion.39
  113.8 0.6 fusion.45
  114.4 0.6 copy-done.9
  115.0 0.6 fusion.35
  116.1 0.6 fusion.34
  116.7 0.6 fusion.33
  117.4 0.6 fusion.32
  118.0 0.6 fusion.31
  118.6 1.1 copy-done.13
  (38 shorter events, 5.8 us)
Async XLA Ops:
  0.6 12.0 %copy-start = (bf16[1536,5,192]{0,2,1:T(8,128)(2,1)S(1)}, bf16[1536,5,192]{0,2,1:T(8,128)(2,1)}, u32[]{:S(2)}) copy-start(bf16[1536,5,192]{0,2,1:T(8,128)(2,1)} %param.7) | copy-start | bytes 8847364
  0.7 0.8 copy-start.7
  11.6 1.0 copy-start.8
  32.6 0.9 copy-start.3
  33.6 1.8 %copy-start.10 = (bf16[768,5,384]{2,0,1:T(8,128)(2,1)S(1)}, bf16[768,5,384]{2,0,1:T(8,128)(2,1)}, u32[]{:S(2)}) copy-start(bf16[768,5,384]{2,0,1:T(8,128)(2,1)} %param.8) | copy-start | bytes 8847364
  62.9 1.0 copy-start.1
  63.9 0.9 copy-start.5
  65.6 2.2 %copy-start.11 = (bf16[768,5,384]{2,0,1:T(8,128)(2,1)S(1)}, bf16[768,5,384]{2,0,1:T(8,128)(2,1)}, u32[]{:S(2)}) copy-start(bf16[768,5,384]{2,0,1:T(8,128)(2,1)} %param.8) | copy-start | bytes 8847364
  70.1 1.3 %copy-start.2 = (bf16[4,544,192]{2,1,0:T(8,128)(2,1)S(1)}, bf16[4,544,192]{2,1,0:T(8,128)(2,1)}, u32[]{:S(2)}) copy-start(bf16[4,544,192]{2,1,0:T(8,128)(2,1)} %copy-done.1) | copy-start | bytes 2506756
  70.1 1.5 %copy-start.4 = (f32[512,384]{1,0:T(8,128)S(1)}, f32[512,384]{1,0:T(8,128)}, u32[]{:S(2)}) copy-start(f32[512,384]{1,0:T(8,128)} %copy-done.3) | copy-start | bytes 2359300
  70.1 1.7 %copy-start.6 = (bf16[4,256,384]{2,1,0:T(8,128)(2,1)S(1)}, bf16[4,256,384]{2,1,0:T(8,128)(2,1)}, u32[]{:S(2)}) copy-start(bf16[4,256,384]{2,1,0:T(8,128)(2,1)} %copy-done.5) | copy-start | bytes 2359300
  113.8 1.2 %copy-start.9 = (bf16[2048,192]{1,0:T(8,128)(2,1)S(1)}, bf16[2048,192]{1,0:T(8,128)(2,1)}, u32[]{:S(2)}) copy-start(bf16[2048,192]{1,0:T(8,128)(2,1)} %copy-done.8) | copy-start | bytes 2359300
  115.0 1.1 copy-start.12
  118.6 1.1 copy-start.13

commit v5 on v4

--- a/solution.py
+++ b/solution.py
@@ -474,7 +474,8 @@
 
 
 def turn_kernel(
-    n, grad_ref, pre_ref, chan_ref, all_ref, pre_seq_ref, slope_seq_ref, up_ref, own, wide, *sems
+    n, w_ref, pre_ref, chan_ref, all_ref, pre_seq_ref, slope_seq_ref, up_ref, own, wide, total,
+    *sems,
 ):
     s, c = lax.axis_index("seq"), lax.axis_index("chan")
     rows = own.shape[0]
@@ -484,16 +485,38 @@
     slope_turn = Turn(n, s, c, slope_own, slope_seq_ref, sems[: len(sems) // 2])
     turn = Turn(n, s, c, own, pre_seq_ref, sems[len(sems) // 2 :])
 
+    width = chan_ref.shape[2]
+    piece = turn.piece
+
     def pre_rows(first):
-        @pl.loop(0, turn.piece // STEP)
+        if first == 2 * piece:
+            slope_turn.forward()
+        if first == 3 * piece:
+            slope_turn.relay()
+        total[...] = jnp.zeros_like(total)
+
+        @pl.loop(0, n)
+        def _(j):
+            window = chan_ref[j, first : first + piece + 2 * EDGE, :].astype(jnp.float32)
+            inputs = pl.ds(pl.multiple_of(j * width, EDGE), width)
+            part = total[...]
+            for k in range(KW):
+                start = EDGE + 2 - k
+                part = part + jnp.dot(
+                    window[start : start + piece].astype(BF16), w_ref[k, inputs, :],
+                    preferred_element_type=jnp.float32,
+                )
+            total[...] = part
+
+        @pl.loop(0, piece // STEP)
         def _(i):
+            local = pl.ds(pl.multiple_of(i * STEP, STEP), STEP)
             at = pl.ds(pl.multiple_of(first + i * STEP, STEP), STEP)
-            grad = 0.5 * pair_add(grad_ref[at, :])
+            grad = 0.5 * pair_add(total[local, :])
             own[at, :] = (grad * gelu_slope(pre_ref[at, :])).astype(BF16)
 
     slope_turn.start()
     turn.start(pre_rows)
-    slope_turn.forward()
     turn.forward()
 
     @pl.loop(0, n)
@@ -505,7 +528,6 @@
             wide[j, pl.ds(1, half, stride=2), :] = value
             up_ref[slot, :, lanes] = wide[j].astype(BF16)
 
-    slope_turn.relay()
     turn.relay()
     slope_turn.finish()
     turn.finish()
@@ -613,14 +635,6 @@
         ],
         dec_part, stem_pad[2 : 2 + rows], targets, pool,
     )
-    slope_pad = jnp.concatenate(
-        [slope_chan[j, EDGE - 2 : EDGE + rows + 2] for j in range(n)], axis=1
-    )
-    up_grad = jnp.zeros((rows, c2), jnp.float32)
-    for k in range(KW):
-        up_grad = up_grad + jnp.dot(
-            slope_pad[4 - k : 4 - k + rows], w_dec[:, k, :], preferred_element_type=jnp.float32
-        )
     pre_seq, slope_seq, up_all = call(
         functools.partial(turn_kernel, n), 3,
         (
@@ -631,9 +645,10 @@
         [
             pltpu.VMEM((rows, c2), BF16),
             pltpu.VMEM((c2 // 128, rows, 128), jnp.float32),
+            pltpu.VMEM((rows // n, c2), jnp.float32),
             *turn_scratch(n), *turn_scratch(n),
         ],
-        up_grad, enc_pre, slope_chan, pool_all,
+        w_dec.transpose(1, 0, 2), enc_pre, slope_chan, pool_all,
     )
     up_all = jnp.pad(up_all.reshape(length, c2), ((2, 2), (0, 0)))
     g_dec = all_rows_grad(slope_seq.reshape(length, c1), up_all)

time: 120 us -> 122 us (1.017); the launches traced: 120 us -> 120 us
  matrix products: 15.4 us -> 12.4 us
  local copies, waits for them, and re-layouts: 13.7 us -> 16.1 us
  Pallas kernels: 89.1 us -> 90.6 us
    unnamed x38, local copies, waits for them, and re-layouts: 11.7 us -> 15.7 us
    dot_general x5 -> x0, matrix products: 2.9 us -> none  [square_shards(): jnp.dot(slope_pad[4 - k:4 - k + rows], w_dec[:, k, :], preferred_element_...]
    squeeze x1 -> x0, local copies, waits for them, and re-layouts: 1.59 us -> none  [square_shards(): slope_chan[j, EDGE - 2:EDGE + rows + 2]]
    pallas_call x4, Pallas kernels: 89.1 us -> 90.6 us  [call(): pl.pallas_call(kernel, out_shape=outs, in_specs=[vmem] * len(operands), o...]
where the time goes in v5:
time: 122 us; the launch traced here: 120 us
  Pallas kernels  90.6 us (74%)
  local copies, waits for them, and re-layouts  16.1 us (13%)
  matrix products  12.4 us (10%)
    pallas_call x4, Pallas kernels, call(): pl.pallas_call(kernel, out_shape=outs, in_specs=[vmem] * len(operands), o...  90.6 us
    unnamed x38, local copies, waits for them, and re-layouts  15.7 us
    dot_general x10, matrix products, all_rows_grad(): lax.dot_general(cotangent, padded[k:k + count], (((0,), (0,)), ((), ())),...  6.11 us
    dot_general x5, matrix products, conv_stack(): lax.dot_general(windows(padded), weight, (((0, 2), (1, 2)), ((), ())), pr...  4.7 us

profile of v5, /device:TPU:0, one launch (start us, length us, event | category | flops | bytes accessed | tf_op | source)
XLA Modules:
  0.0 120.3 jit_solution(13347923710229504977)
XLA Ops:
  0.7 0.8 copy-done.9
  1.5 7.3 %shard_map.76 = s32[4,4,128]{2,1,0:T(4,128)S(1)} custom-call(s32[4,128]{1,0:T(4,128)S(1)} %bitcast.154), custom_call_target="tpu_custom_call" | custom-call | tf_op jit(solution)/shard_map/pallas_call | solution.py:542
  8.9 1.1 copy.34.target_ref
  10.0 1.6 %fusion.5 = bf16[2048,192]{1,0:T(8,128)(2,1)S(1)} fusion(s32[5,2048]{1,0:T(8,128)S(1)} %stack.128, bf16[192,5,4]{0,2,1:T(4,128)(2,1)} %param.6), kind=kOutput, calls=%fused_computation.8 | convolution fusion | flops 19308544 | bytes 835072 | tf_op jit(solution)/shard_map/dot_general | solution.py:595
  12.7 1.8 %fusion.part_ref = bf16[512,1536]{1,0:T(8,128)(2,1)S(1)} fusion(bf16[5,512,192]{2,1,0:T(8,128)(2,1)S(1)} %fusion.64, bf16[1536,5,192]{0,2,1:T(8,128)(2,1)S(1)} %copy-done), kind=kOutput, calls=%fused_computation.2 | convolution fusion | flops 1510735872 | bytes 5505024 | tf_op jit(solution)/shard_map/dot_general | solution.py:564
  14.5 18.1 %shard_map.77 = (f32[512,384]{1,0:T(8,128)S(1)}, bf16[544,384]{1,0:T(8,128)(2,1)S(1)}, bf16[256,384]{1,0:T(8,128)(2,1)S(1)}) custom-call(bf16[512,1536]{1,0:T(8,128)(2,1)S(1)} %fusion.part_ref), custom_call_target="tpu_custom_call" | custom-call | tf_op jit(solution)/shard_map/pallas_call | solution.py:542
  32.6 0.9 copy-done.5
  34.1 1.3 %copy-done.1 = bf16[768,5,384]{2,0,1:T(8,128)(2,1)S(1)} copy-done((bf16[768,5,384]{2,0,1:T(8,128)(2,1)S(1)}, bf16[768,5,384]{2,0,1:T(8,128)(2,1)}, u32[]{:S(2)}) %copy-start.1) | copy-done | bytes 2949144
  35.5 0.7 fusion.48
  36.2 0.7 fusion.49
  36.9 0.7 fusion.50
  37.6 0.7 fusion.51
  38.6 24.3 %shard_map.78 = (bf16[512,192]{1,0:T(8,128)(2,1)S(1)}, bf16[4,544,192]{2,1,0:T(8,128)(2,1)S(1)}, bf16[4,256,384]{2,1,0:T(8,128)(2,1)S(1)}) custom-call(bf16[4,512,192]{2,1,0:T(8,128)(2,1)S(1)} %pad_maximum_fusion.part_ref, bf16[512,192]{1,0:T(8,128)(2,1)S(1)} %get-tuple-element.28.stem_ref, bf16[512,192]{1,0:T(8,128)(2,1)S(1)} %copy.34.target_ref, ...), custom_call_target="tpu_custom_call" | custom-call | tf_op jit(solution)/shard_map/pallas_call | solution.py:542
  62.9 1.0 copy-done.3
  63.9 0.9 copy-done.7
  64.8 0.8 copy.36
  65.6 1.8 %copy-done.2 = bf16[768,5,384]{2,0,1:T(8,128)(2,1)S(1)} copy-done((bf16[768,5,384]{2,0,1:T(8,128)(2,1)S(1)}, bf16[768,5,384]{2,0,1:T(8,128)(2,1)}, u32[]{:S(2)}) %copy-start.2) | copy-done | bytes 2949144
  67.4 1.2 %copy-done.4 = bf16[4,544,192]{2,1,0:T(8,128)(2,1)S(1)} copy-done((bf16[4,544,192]{2,1,0:T(8,128)(2,1)S(1)}, bf16[4,544,192]{2,1,0:T(8,128)(2,1)}, u32[]{:S(2)}) %copy-start.4) | copy-done | bytes 835608
  68.7 1.1 copy-done.6
  69.8 1.1 copy-done.8
  70.9 41.0 %shard_map.79 = (bf16[4,512,384]{2,1,0:T(8,128)(2,1)S(1)}, bf16[4,512,192]{2,1,0:T(8,128)(2,1)S(1)}, bf16[4,512,384]{2,1,0:T(8,128)(2,1)S(1)}) custom-call(bf16[5,768,384]{2,1,0:T(8,128)(2,1)S(1)} %bitcast.151, f32[512,384]{1,0:T(8,128)S(1)} %copy-done.6, bf16[4,544,192]{2,1,0:T(8,128)(2,1)S(1)} %copy-done.4, bf16[4,256,384]{2,1,0:T(8,128)(2,1)S(1)} %copy-done.8), custom_call_target="tpu_custom_call" | custom-call | tf_op jit(solution)/shard_map/pallas_call | solution.py:542
  111.9 0.6 fusion.21
  112.5 0.6 fusion.27
  113.2 0.6 fusion.30
  113.8 0.6 fusion.39
  115.0 0.6 copy-done.11
  115.6 0.6 fusion.35
  116.7 0.6 fusion.34
  117.3 0.6 fusion.33
  118.0 0.6 fusion.32
  118.6 0.6 fusion.31
  119.2 1.1 copy-done.13
  (31 shorter events, 3.1 us)
Async XLA Ops:
  0.6 12.0 %copy-start = (bf16[1536,5,192]{0,2,1:T(8,128)(2,1)S(1)}, bf16[1536,5,192]{0,2,1:T(8,128)(2,1)}, u32[]{:S(2)}) copy-start(bf16[1536,5,192]{0,2,1:T(8,128)(2,1)} %param.7) | copy-start | bytes 8847364
  0.7 0.8 copy-start.9
  11.6 1.0 copy-start.10
  32.6 0.9 copy-start.5
  33.6 1.8 %copy-start.1 = (bf16[768,5,384]{2,0,1:T(8,128)(2,1)S(1)}, bf16[768,5,384]{2,0,1:T(8,128)(2,1)}, u32[]{:S(2)}) copy-start(bf16[768,5,384]{2,0,1:T(8,128)(2,1)} %param.8) | copy-start | bytes 8847364
  62.9 1.0 copy-start.3
  63.9 0.9 copy-start.7
  65.6 1.8 %copy-start.2 = (bf16[768,5,384]{2,0,1:T(8,128)(2,1)S(1)}, bf16[768,5,384]{2,0,1:T(8,128)(2,1)}, u32[]{:S(2)}) copy-start(bf16[768,5,384]{2,0,1:T(8,128)(2,1)} %param.8) | copy-start | bytes 8847364
  67.4 1.2 %copy-start.4 = (bf16[4,544,192]{2,1,0:T(8,128)(2,1)S(1)}, bf16[4,544,192]{2,1,0:T(8,128)(2,1)}, u32[]{:S(2)}) copy-start(bf16[4,544,192]{2,1,0:T(8,128)(2,1)} %copy-done.3) | copy-start | bytes 2506756
  68.7 1.1 copy-start.6
  69.8 1.1 copy-start.8
  114.4 1.2 %copy-start.11 = (bf16[2048,192]{1,0:T(8,128)(2,1)S(1)}, bf16[2048,192]{1,0:T(8,128)(2,1)}, u32[]{:S(2)}) copy-start(bf16[2048,192]{1,0:T(8,128)(2,1)} %copy-done.10) | copy-start | bytes 2359300
  115.6 1.1 copy-start.12
  119.2 1.1 copy-start.13

commit v6 on v5

--- a/solution.py
+++ b/solution.py
@@ -480,7 +480,6 @@
     s, c = lax.axis_index("seq"), lax.axis_index("chan")
     rows = own.shape[0]
     half, up_width = all_ref.shape[1:]
-    greet(whole_group(n, s, c))
     slope_own = chan_ref.at[c, pl.ds(EDGE, rows)]
     slope_turn = Turn(n, s, c, slope_own, slope_seq_ref, sems[: len(sems) // 2])
     turn = Turn(n, s, c, own, pre_seq_ref, sems[len(sems) // 2 :])
@@ -531,6 +530,20 @@
     turn.relay()
     slope_turn.finish()
     turn.finish()
+
+
+def decoder_kernel(
+    n, scale, part_ref, stem_ref, target_ref, pool_ref, w_ref, pre_ref,
+    pred_ref, pre_seq_ref, slope_seq_ref, up_ref, chan, pools, held, pair, own, wide, total, *sems
+):
+    slope_kernel(
+        n, scale, part_ref, stem_ref, target_ref, pool_ref, pred_ref, chan, pools, held, pair,
+        *sems[:12],
+    )
+    turn_kernel(
+        n, w_ref, pre_ref, chan, pools, pre_seq_ref, slope_seq_ref, up_ref, own, wide, total,
+        *sems[12:],
+    )
 
 
 def turn_scratch(n):
@@ -619,36 +632,28 @@
     dec_part = jnp.stack(
         [conv_stack(up_pad, w_dec[j * c1 : (j + 1) * c1]).astype(BF16) for j in range(n)]
     )
-    pred, slope_chan, pool_all = call(
-        functools.partial(slope_kernel, n, 1.0 / math.sqrt(length)), 2,
+    pred, pre_seq, slope_seq, up_all = call(
+        functools.partial(decoder_kernel, n, 1.0 / math.sqrt(length)), 2,
         (
             struct((rows, c1), BF16),
-            struct((n, rows + 2 * EDGE, c1), BF16),
-            struct((n, half, c2), BF16),
-        ),
-        [
-            pltpu.VMEM((n - 1, rows, c1), BF16),
-            pltpu.VMEM((rows, c1), BF16),
-            dma(3 * CHUNKS), dma(3 * CHUNKS), dma(3 * CHUNKS), dma(3 * CHUNKS),
-            dma(n), dma(n), dma(n), dma(n), dma(n), dma(n), dma(n),
-            pltpu.SemaphoreType.DMA,
-        ],
-        dec_part, stem_pad[2 : 2 + rows], targets, pool,
-    )
-    pre_seq, slope_seq, up_all = call(
-        functools.partial(turn_kernel, n), 3,
-        (
             struct((n, rows, c2), BF16),
             struct((n, rows, c1), BF16),
             struct((n, rows, c2), BF16),
         ),
         [
+            pltpu.VMEM((n, rows + 2 * EDGE, c1), BF16),
+            pltpu.VMEM((n, half, c2), BF16),
+            pltpu.VMEM((n - 1, rows, c1), BF16),
+            pltpu.VMEM((rows, c1), BF16),
             pltpu.VMEM((rows, c2), BF16),
             pltpu.VMEM((c2 // 128, rows, 128), jnp.float32),
             pltpu.VMEM((rows // n, c2), jnp.float32),
+            dma(3 * CHUNKS), dma(3 * CHUNKS), dma(3 * CHUNKS), dma(3 * CHUNKS),
+            dma(n), dma(n), dma(n), dma(n), dma(n), dma(n), dma(n),
+            pltpu.SemaphoreType.DMA,
             *turn_scratch(n), *turn_scratch(n),
         ],
-        w_dec.transpose(1, 0, 2), enc_pre, slope_chan, pool_all,
+        dec_part, stem_pad[2 : 2 + rows], targets, pool, w_dec.transpose(1, 0, 2), enc_pre,
     )
     up_all = jnp.pad(up_all.reshape(length, c2), ((2, 2), (0, 0)))
     g_dec = all_rows_grad(slope_seq.reshape(length, c1), up_all)

time: 122 us -> 114 us (0.934); the launches traced: 120 us -> 114 us
  local copies, waits for them, and re-layouts: 16.1 us -> 11.2 us
  Pallas kernels: 90.6 us -> 87.5 us
  matrix products: 12.4 us -> 14.3 us
    unnamed x38 -> x36, local copies, waits for them, and re-layouts: 15.7 us -> 10.9 us
    pallas_call x4 -> x3, Pallas kernels: 90.6 us -> 87.5 us  [call(): pl.pallas_call(kernel, out_shape=outs, in_specs=[vmem] * len(operands), o...]
    dot_general x10, matrix products: 6.11 us -> 7.96 us  [all_rows_grad(): lax.dot_general(cotangent, padded[k:k + count], (((0,), (0,)), ((), ())),...]
where the time goes in v6:
time: 114 us
  Pallas kernels  87.5 us (77%)
  matrix products  14.3 us (13%)
  local copies, waits for them, and re-layouts  11.2 us (10%)
    pallas_call x3, Pallas kernels, call(): pl.pallas_call(kernel, out_shape=outs, in_specs=[vmem] * len(operands), o...  87.5 us
    unnamed x36, local copies, waits for them, and re-layouts  10.9 us
    dot_general x10, matrix products, all_rows_grad(): lax.dot_general(cotangent, padded[k:k + count], (((0,), (0,)), ((), ())),...  7.96 us
    dot_general x5, matrix products, conv_stack(): lax.dot_general(windows(padded), weight, (((0, 2), (1, 2)), ((), ())), pr...  4.73 us

profile of v6, /device:TPU:0, one launch (start us, length us, event | category | flops | bytes accessed | tf_op | source)
XLA Modules:
  0.0 114.2 jit_solution(9137651092722549817)
XLA Ops:
  0.7 0.8 copy-done.6
  1.5 7.3 %shard_map.76 = s32[4,4,128]{2,1,0:T(4,128)S(1)} custom-call(s32[4,128]{1,0:T(4,128)S(1)} %bitcast.154), custom_call_target="tpu_custom_call" | custom-call | tf_op jit(solution)/shard_map/pallas_call | solution.py:555
  8.9 1.1 copy.34.target_ref
  10.0 1.6 %fusion.5 = bf16[2048,192]{1,0:T(8,128)(2,1)S(1)} fusion(s32[5,2048]{1,0:T(8,128)S(1)} %stack.128, bf16[192,5,4]{0,2,1:T(4,128)(2,1)} %param.6), kind=kOutput, calls=%fused_computation.8 | convolution fusion | flops 19308544 | bytes 835072 | tf_op jit(solution)/shard_map/dot_general | solution.py:608
  12.0 0.6 copy-done.9
  12.7 1.8 %fusion.part_ref = bf16[512,1536]{1,0:T(8,128)(2,1)S(1)} fusion(bf16[5,512,192]{2,1,0:T(8,128)(2,1)S(1)} %fusion.64, bf16[1536,5,192]{0,2,1:T(8,128)(2,1)S(1)} %copy-done), kind=kOutput, calls=%fused_computation.2 | convolution fusion | flops 1510735872 | bytes 5505024 | tf_op jit(solution)/shard_map/dot_general | solution.py:577
  14.5 18.1 %shard_map.77 = (f32[512,384]{1,0:T(8,128)S(1)}, bf16[544,384]{1,0:T(8,128)(2,1)S(1)}, bf16[256,384]{1,0:T(8,128)(2,1)S(1)}) custom-call(bf16[512,1536]{1,0:T(8,128)(2,1)S(1)} %fusion.part_ref), custom_call_target="tpu_custom_call" | custom-call | tf_op jit(solution)/shard_map/pallas_call | solution.py:555
  33.0 0.1 bitcast_dynamic-update-slice_fusion.1
  33.2 1.3 %copy-done.5 = bf16[768,5,384]{2,0,1:T(8,128)(2,1)S(1)} copy-done((bf16[768,5,384]{2,0,1:T(8,128)(2,1)S(1)}, bf16[768,5,384]{2,0,1:T(8,128)(2,1)}, u32[]{:S(2)}) %copy-start.5) | copy-done | bytes 2949144
  34.6 0.7 fusion.48
  35.3 0.7 fusion.49
  36.0 0.7 fusion.50
  36.8 0.7 fusion.51
  37.5 0.2 pad_maximum_fusion.part_ref
  37.7 62.1 %shard_map.78 = (bf16[512,192]{1,0:T(8,128)(2,1)S(1)}, bf16[4,512,384]{2,1,0:T(8,128)(2,1)S(1)}, bf16[4,512,192]{2,1,0:T(8,128)(2,1)S(1)}, bf16[4,512,384]{2,1,0:T(8,128)(2,1)S(1)}) custom-call(bf16[4,512,192]{2,1,0:T(8,128)(2,1)S(1)} %pad_maximum_fusion.part_ref, bf16[512,192]{1,0:T(8,128)(2,1)S(1)} %get-tuple-element.24.stem_ref, ...), custom_call_target="tpu_custom_call" | custom-call | tf_op jit(solution)/shard_map/pallas_call | solution.py:555
  99.8 1.2 %copy-done.1 = bf16[4,512,384]{2,1,0:T(8,128)(2,1)} copy-done((bf16[4,512,384]{2,1,0:T(8,128)(2,1)}, bf16[4,512,384]{2,1,0:T(8,128)(2,1)S(1)}, u32[]{:S(2)}) %copy-start.1) | copy-done | bytes 1572888
  101.0 1.0 copy-done.3
  102.0 1.1 %copy-done.7 = bf16[4,512,384]{2,1,0:T(8,128)(2,1)} copy-done((bf16[4,512,384]{2,1,0:T(8,128)(2,1)}, bf16[4,512,384]{2,1,0:T(8,128)(2,1)S(1)}, u32[]{:S(2)}) %copy-start.7) | copy-done | bytes 1572888
  103.1 0.8 copy.36
  103.9 2.5 %fusion.35 = f32[384,5,192]{0,2,1:T(8,128)S(1)} fusion(bf16[2048,384]{1,0:T(8,128)(2,1)} %bitcast.155, bf16[2048,192]{1,0:T(8,128)(2,1)} %copy-done.9), kind=kOutput, calls=%fused_computation.40 | convolution fusion | flops 301989888 | bytes 2654208 | tf_op jit(solution)/shard_map/dot_general | solution.py:585
  106.4 0.6 fusion.34
  107.1 0.6 fusion.33
  107.7 0.6 fusion.32
  108.3 0.6 fusion.31
  109.0 0.8 copy-done.2
  109.7 0.3 copy-done.4
  110.0 0.6 fusion.21
  110.6 0.6 fusion.27
  111.2 0.6 fusion.30
  111.8 0.6 fusion.39
  112.5 0.6 fusion.45
  113.1 1.1 copy-done.11
  (28 shorter events, 1.0 us)
Async XLA Ops:
  0.6 12.0 %copy-start = (bf16[1536,5,192]{0,2,1:T(8,128)(2,1)S(1)}, bf16[1536,5,192]{0,2,1:T(8,128)(2,1)}, u32[]{:S(2)}) copy-start(bf16[1536,5,192]{0,2,1:T(8,128)(2,1)} %param.7) | copy-start | bytes 8847364
  0.7 0.8 copy-start.6
  11.6 1.0 copy-start.9
  32.7 1.8 %copy-start.5 = (bf16[768,5,384]{2,0,1:T(8,128)(2,1)S(1)}, bf16[768,5,384]{2,0,1:T(8,128)(2,1)}, u32[]{:S(2)}) copy-start(bf16[768,5,384]{2,0,1:T(8,128)(2,1)} %param.8) | copy-start | bytes 8847364
  99.8 1.2 %copy-start.1 = (bf16[4,512,384]{2,1,0:T(8,128)(2,1)}, bf16[4,512,384]{2,1,0:T(8,128)(2,1)S(1)}, u32[]{:S(2)}) copy-start(bf16[4,512,384]{2,1,0:T(8,128)(2,1)S(1)} %get-tuple-element.16) | copy-start | bytes 4718596
  101.0 1.0 copy-start.3
  102.0 1.1 %copy-start.7 = (bf16[4,512,384]{2,1,0:T(8,128)(2,1)}, bf16[4,512,384]{2,1,0:T(8,128)(2,1)S(1)}, u32[]{:S(2)}) copy-start(bf16[4,512,384]{2,1,0:T(8,128)(2,1)S(1)} %get-tuple-element.14) | copy-start | bytes 4718596
  103.9 2.5 %copy-start.8 = (bf16[4,512,384]{2,1,0:T(8,128)(2,1)S(1)}, bf16[4,512,384]{2,1,0:T(8,128)(2,1)}, u32[]{:S(2)}) copy-start(bf16[4,512,384]{2,1,0:T(8,128)(2,1)} %copy-done.7) | copy-start | bytes 4718596
  103.9 2.5 %copy-start.10 = (bf16[2048,192]{1,0:T(8,128)(2,1)S(1)}, bf16[2048,192]{1,0:T(8,128)(2,1)}, u32[]{:S(2)}) copy-start(bf16[2048,192]{1,0:T(8,128)(2,1)} %copy-done.9) | copy-start | bytes 2359300
  108.3 1.4 %copy-start.2 = (bf16[4,512,384]{2,1,0:T(8,128)(2,1)S(1)}, bf16[4,512,384]{2,1,0:T(8,128)(2,1)}, u32[]{:S(2)}) copy-start(bf16[4,512,384]{2,1,0:T(8,128)(2,1)} %copy-done.1) | copy-start | bytes 4718596
  108.3 1.7 %copy-start.4 = (bf16[4,512,192]{2,1,0:T(8,128)(2,1)S(1)}, bf16[4,512,192]{2,1,0:T(8,128)(2,1)}, u32[]{:S(2)}) copy-start(bf16[4,512,192]{2,1,0:T(8,128)(2,1)} %copy-done.3) | copy-start | bytes 2359300
  110.0 1.2 %copy-start.12 = (f32[384,5,192]{0,2,1:T(8,128)}, f32[384,5,192]{0,2,1:T(8,128)S(1)}, u32[]{:S(2)}) copy-start(f32[384,5,192]{0,2,1:T(8,128)S(1)} %fusion.31) | copy-start | bytes 4423684
  113.1 1.1 copy-start.11
